TPU v7x, 32 devices: a whole 2x2x4 slice. The times are simulated.
32 devices in a mesh: dp: 16 (over z, y, x), fsdp: 2 (over core).
Axes of the slice: x: 2, y: 2, z: 4, core: 2. Of those that a mesh axis runs over, the one named last changes fastest.
Arguments:
- tokens: bfloat16 [64, 512, 768], P(('dp', 'fsdp')), may hold values from -6 to 6
- cotangent: bfloat16 [64, 80, 768], P(('dp', 'fsdp')), may hold values from -6 to 6
- positions: int32 [64, 80], P(('dp', 'fsdp')), may hold values from 0 to 511, as said below
- counts: int32 [64], P(('dp', 'fsdp')), may hold values from 40 to 80
- query_key_value_weight: bfloat16 [2, 768, 2304], P(None, ('dp', 'fsdp')), may hold values from -0.21875 to 0.21875
- attention_output_weight: bfloat16 [2, 768, 768], P(None, ('dp', 'fsdp')), may hold values from -0.625 to 0.625
- feedforward_input_weight: bfloat16 [2, 768, 3072], P(None, ('dp', 'fsdp')), may hold values from -0.21875 to 0.21875
- feedforward_input_bias: bfloat16 [2, 3072], P(None, ('dp', 'fsdp')), may hold values from -3 to 3
- feedforward_output_weight: bfloat16 [2, 3072, 768], P(None, ('dp', 'fsdp')), may hold values from -0.109375 to 0.109375
- small: bfloat16 [2, 768, 24], P(None, ('dp', 'fsdp'))
- query_up_weight: float32 [2, 8, 768], replicated, may hold values from -1.2 to 1.2
- value_up_weight: float32 [2, 8, 768], replicated, may hold values from -1.2 to 1.2
Outputs:
- activations: bfloat16 [64, 512, 768], P(('dp', 'fsdp'))
- d_tokens: float32 [64, 512, 768], P(('dp', 'fsdp'))
- query_up_gradient: float32 [2, 8, 768], replicated
- value_up_gradient: float32 [2, 8, 768], replicated
Inputs may be any that keep to these rules, and one draw needn't show every extreme that they name: In each sequence the 80 entries are distinct positions; entry m is used where m < counts of that sequence.
All inputs are finite; a program needn't handle non-finite values.
Results may differ from a plain program's by a relative error of at most 0.03.
Values may be sent and summed in bfloat16 or wider, within the bound.
No kernel may reach another device: no remote copies, remote signals or barrier semaphores. Data moves between devices by JAX's collectives and lax.ppermute only.
A program may use at most 256 MiB of HBM per device.

v0:
```python
import jax
import jax.numpy as jnp
from jax import lax
from jax.sharding import PartitionSpec as P

MODEL_WIDTH = 768
H = 12
HD = 64
ADAPTER_RANK = 8
ENCODER_LAYERS = 2
LEN = 512
MAXM = 80


EPSILON = 1e-05


def layer_norm(value, norm_gain, norm_shift):
    average = jnp.mean(value, axis=-1, keepdims=True)
    centred = value - average
    spread = jnp.mean(centred * centred, axis=-1, keepdims=True)
    return centred * lax.rsqrt(spread + EPSILON) * norm_gain + norm_shift


def gelu_exact(value):
    return jax.nn.gelu(value, approximate=False)


def matrix_multiply(left, right):
    return jnp.dot(left, right, preferred_element_type=jnp.float32)


def transposed_multiply(left, right):
    return lax.dot_general(
        left, right, (((1,), (1,)), ((), ())), preferred_element_type=jnp.float32
    )


def leading_axis_contract(left, right):
    return lax.dot_general(
        left, right, (((0,), (0,)), ((), ())), preferred_element_type=jnp.float32
    )


def fetch_forward(layer_qkv, layer_o, layer_in, layer_bias, layer_out, layer_small):
    return (
        lax.all_gather(layer_qkv, ("dp", "fsdp"), axis=0, tiled=True),
        lax.all_gather(layer_o, ("dp", "fsdp"), axis=0, tiled=True),
        lax.all_gather(layer_in, ("dp", "fsdp"), axis=0, tiled=True),
        lax.all_gather(layer_bias, ("dp", "fsdp"), axis=0, tiled=True),
        lax.all_gather(layer_out, ("dp", "fsdp"), axis=0, tiled=True),
        lax.all_gather(layer_small, ("dp", "fsdp"), axis=0, tiled=True),
    )


def fetch_backward(layer_qkv, layer_o, layer_in, layer_bias, layer_out, layer_small):
    return (
        lax.all_gather(layer_qkv, ("dp", "fsdp"), axis=0, tiled=True),
        lax.all_gather(layer_o, ("dp", "fsdp"), axis=0, tiled=True),
        lax.all_gather(layer_in, ("dp", "fsdp"), axis=0, tiled=True),
        lax.all_gather(layer_bias, ("dp", "fsdp"), axis=0, tiled=True),
        lax.all_gather(layer_out, ("dp", "fsdp"), axis=0, tiled=True),
        lax.all_gather(layer_small, ("dp", "fsdp"), axis=0, tiled=True),
    )


def attend(packed_projection):
    heads_view = packed_projection.reshape(LEN, 3, H, HD)
    query_rows = heads_view[:, 0]
    key_rows = heads_view[:, 1]
    value_matrix_rows = heads_view[:, 2]
    scores = (
        jnp.einsum("qhd,khd->hqk", query_rows, key_rows, preferred_element_type=jnp.float32) * 0.125
    )
    row_max = jnp.max(scores, axis=-1, keepdims=True)
    powers = jnp.exp(scores - row_max)
    row_sum = jnp.sum(powers, axis=-1, keepdims=True)
    soft_probs = (powers / row_sum).astype(jnp.bfloat16)
    context = jnp.einsum(
        "hqk,khd->qhd", soft_probs, value_matrix_rows, preferred_element_type=jnp.float32
    )
    return (
        context.reshape(LEN, H * HD).astype(jnp.bfloat16),
        (row_max + jnp.log(row_sum))[:, :, 0],
    )


def attend_back(element):
    packed_projection, logsumexp_total, d_context = element
    heads_view = packed_projection.reshape(LEN, 3, H, HD)
    query_rows = heads_view[:, 0]
    key_rows = heads_view[:, 1]
    value_matrix_rows = heads_view[:, 2]
    grad_view = d_context.reshape(LEN, H, HD)
    scores = (
        jnp.einsum("qhd,khd->hqk", query_rows, key_rows, preferred_element_type=jnp.float32) * 0.125
    )
    soft_probs = jnp.exp(scores - logsumexp_total[:, :, None])
    d_probs = jnp.einsum(
        "qhd,khd->hqk", grad_view, value_matrix_rows, preferred_element_type=jnp.float32
    )
    d_scores = (
        soft_probs * (d_probs - jnp.sum(soft_probs * d_probs, axis=-1, keepdims=True))
    ).astype(jnp.bfloat16)
    d_queries = (
        jnp.einsum("hqk,khd->qhd", d_scores, key_rows, preferred_element_type=jnp.float32) * 0.125
    ).astype(jnp.bfloat16)
    d_keys = (
        jnp.einsum("hqk,qhd->khd", d_scores, query_rows, preferred_element_type=jnp.float32) * 0.125
    ).astype(jnp.bfloat16)
    d_values = jnp.einsum(
        "hqk,qhd->khd",
        soft_probs.astype(jnp.bfloat16),
        grad_view,
        preferred_element_type=jnp.float32,
    ).astype(jnp.bfloat16)
    return jnp.stack([d_queries, d_keys, d_values], axis=1).reshape(LEN, 3 * H * HD)


def layer_forward_pass(hidden_state, collected_rows, query_adapter_output, value_adapter_output):
    (
        query_key_value_weight,
        attention_output_weight,
        feedforward_input_weight,
        feedforward_input_bias,
        feedforward_output_weight,
        small,
    ) = collected_rows
    params = small.astype(jnp.float32)
    rounded_input = hidden_state.astype(jnp.bfloat16)
    adapter_down_weight = matrix_multiply(rounded_input, small[:, 8 : 8 + 2 * ADAPTER_RANK]).astype(
        jnp.bfloat16
    )
    adapter_up_weight = jnp.concatenate(
        [
            2.0
            * matrix_multiply(
                adapter_down_weight[:, :ADAPTER_RANK], query_adapter_output.astype(jnp.bfloat16)
            ),
            jnp.zeros_like(hidden_state),
            2.0
            * matrix_multiply(
                adapter_down_weight[:, ADAPTER_RANK:], value_adapter_output.astype(jnp.bfloat16)
            ),
        ],
        axis=1,
    )
    bias_vector_row = jnp.concatenate([params[:, 0], jnp.zeros_like(params[:, 0]), params[:, 1]])
    packed_projection = (
        matrix_multiply(rounded_input, query_key_value_weight) + bias_vector_row + adapter_up_weight
    ).astype(jnp.bfloat16)
    context, logsumexp_total = lax.map(attend, packed_projection.reshape(-1, LEN, 3 * MODEL_WIDTH))
    context = context.reshape(-1, MODEL_WIDTH)
    leading_partial_sum = hidden_state + (
        matrix_multiply(context, attention_output_weight) + params[:, 2]
    )
    normed = layer_norm(leading_partial_sum, params[:, 3], params[:, 4])
    preactivation_input = matrix_multiply(
        normed.astype(jnp.bfloat16), feedforward_input_weight
    ) + feedforward_input_bias.astype(jnp.float32)
    trailing_partial_sum = normed + (
        matrix_multiply(
            gelu_exact(preactivation_input).astype(jnp.bfloat16), feedforward_output_weight
        )
        + params[:, 5]
    )
    layer_output = layer_norm(trailing_partial_sum, params[:, 6], params[:, 7])
    return (
        layer_output,
        (
            packed_projection,
            adapter_down_weight,
            logsumexp_total,
            leading_partial_sum,
            preactivation_input,
            trailing_partial_sum,
        ),
    )


def layer_backward_pass(
    incoming_gradient, saved_state, collected_rows, query_adapter_output, value_adapter_output
):
    (
        query_key_value_weight,
        attention_output_weight,
        feedforward_input_weight,
        feedforward_input_bias,
        feedforward_output_weight,
        small,
    ) = collected_rows
    params = small.astype(jnp.float32)
    (
        packed_projection,
        adapter_down_weight,
        logsumexp_total,
        leading_partial_sum,
        preactivation_input,
        trailing_partial_sum,
    ) = saved_state
    unused_second, second_back = jax.vjp(
        lambda value: layer_norm(value, params[:, 6], params[:, 7]), trailing_partial_sum
    )
    d_second = second_back(incoming_gradient)[0]
    d_act = transposed_multiply(d_second.astype(jnp.bfloat16), feedforward_output_weight)
    unused_gelu, gelu_back = jax.vjp(gelu_exact, preactivation_input)
    d_pre = gelu_back(d_act)[0].astype(jnp.bfloat16)
    d_normed = d_second + transposed_multiply(d_pre, feedforward_input_weight)
    unused_first, first_back = jax.vjp(
        lambda value: layer_norm(value, params[:, 3], params[:, 4]), leading_partial_sum
    )
    d_first = first_back(d_normed)[0]
    d_context = transposed_multiply(d_first.astype(jnp.bfloat16), attention_output_weight).astype(
        jnp.bfloat16
    )
    d_packed = lax.map(
        attend_back,
        (
            packed_projection.reshape(-1, LEN, 3 * MODEL_WIDTH),
            logsumexp_total,
            d_context.reshape(-1, LEN, MODEL_WIDTH),
        ),
    )
    d_packed = d_packed.reshape(-1, 3 * MODEL_WIDTH)
    query_adapter_gradient = d_packed[:, :MODEL_WIDTH]
    value_adapter_gradient = d_packed[:, 2 * MODEL_WIDTH :]
    d_down = jnp.concatenate(
        [
            2.0
            * transposed_multiply(
                query_adapter_gradient, query_adapter_output.astype(jnp.bfloat16)
            ),
            2.0
            * transposed_multiply(
                value_adapter_gradient, value_adapter_output.astype(jnp.bfloat16)
            ),
        ],
        axis=1,
    ).astype(jnp.bfloat16)
    query_gradient_total = 2.0 * leading_axis_contract(
        adapter_down_weight[:, :ADAPTER_RANK], query_adapter_gradient
    )
    value_gradient_total = 2.0 * leading_axis_contract(
        adapter_down_weight[:, ADAPTER_RANK:], value_adapter_gradient
    )
    d_input = (
        d_first
        + transposed_multiply(d_packed, query_key_value_weight)
        + transposed_multiply(d_down, small[:, 8 : 8 + 2 * ADAPTER_RANK])
    )
    return (d_input, query_gradient_total, value_gradient_total)


def on_device(
    tokens,
    cotangent,
    positions,
    counts,
    query_key_value_weight,
    attention_output_weight,
    feedforward_input_weight,
    feedforward_input_bias,
    feedforward_output_weight,
    small,
    query_up_weight,
    value_up_weight,
):
    hidden_state = tokens.reshape(-1, MODEL_WIDTH).astype(jnp.float32)
    saved_state_stack = []
    gathered_all = []
    for layer_index in range(ENCODER_LAYERS):
        collected_rows = fetch_forward(
            query_key_value_weight[layer_index],
            attention_output_weight[layer_index],
            feedforward_input_weight[layer_index],
            feedforward_input_bias[layer_index],
            feedforward_output_weight[layer_index],
            small[layer_index],
        )
        hidden_state, saved_state = layer_forward_pass(
            hidden_state, collected_rows, query_up_weight[layer_index], value_up_weight[layer_index]
        )
        saved_state_stack.append(saved_state)
        gathered_all.append(collected_rows)
    activations = hidden_state.astype(jnp.bfloat16).reshape(tokens.shape)
    is_live = jnp.arange(MAXM)[None, :] < counts[:, None]
    indicator_matrix = (
        (positions[:, :, None] == jnp.arange(LEN)[None, None, :]) & is_live[:, :, None]
    ).astype(jnp.bfloat16)
    incoming_gradient = jnp.einsum(
        "nkw,nkq->nwq", indicator_matrix, cotangent, preferred_element_type=jnp.float32
    ).reshape(-1, MODEL_WIDTH)
    query_gradient_stack = [None] * ENCODER_LAYERS
    value_gradient_stack = [None] * ENCODER_LAYERS
    for layer_index in reversed(range(ENCODER_LAYERS)):
        collected_rows = fetch_backward(
            query_key_value_weight[layer_index],
            attention_output_weight[layer_index],
            feedforward_input_weight[layer_index],
            feedforward_input_bias[layer_index],
            feedforward_output_weight[layer_index],
            small[layer_index],
        )
        incoming_gradient, query_gradient_total, value_gradient_total = layer_backward_pass(
            incoming_gradient,
            saved_state_stack[layer_index],
            collected_rows,
            query_up_weight[layer_index],
            value_up_weight[layer_index],
        )
        query_gradient_total, value_gradient_total = lax.psum(
            (query_gradient_total, value_gradient_total), ("dp", "fsdp")
        )
        query_gradient_stack[layer_index] = query_gradient_total
        value_gradient_stack[layer_index] = value_gradient_total
    query_up_gradient = jnp.stack(query_gradient_stack)
    value_up_gradient = jnp.stack(value_gradient_stack)
    return (
        activations,
        incoming_gradient.reshape(tokens.shape),
        query_up_gradient,
        value_up_gradient,
    )


def solution(mesh):
    in_specs = (
        P(("dp", "fsdp"), None, None),
        P(("dp", "fsdp"), None, None),
        P(("dp", "fsdp"), None),
        P(("dp", "fsdp")),
        P(None, ("dp", "fsdp"), None),
        P(None, ("dp", "fsdp"), None),
        P(None, ("dp", "fsdp"), None),
        P(None, ("dp", "fsdp")),
        P(None, ("dp", "fsdp"), None),
        P(None, ("dp", "fsdp"), None),
        P(),
        P(),
    )
    out_specs = (P(("dp", "fsdp"), None, None), P(("dp", "fsdp"), None, None), P(), P())
    return jax.shard_map(
        on_device, mesh=mesh, in_specs=in_specs, out_specs=out_specs, check_vma=False
    )
```

profile of v0, /device:TPU:0, one launch (start us, length us, event | category | flops | bytes accessed | tf_op | source)
XLA Modules:
  0.0 912.5 jit_solution(5408790582590353400)
XLA Ops:
  17.6 44.0 %all-gather.7 = bf16[1,768,24]{2,1,0:T(8,128)(2,1)S(1)} all-gather(bf16[1,24,24]{2,1,0:T(8,128)(2,1)S(1)} %get-tuple-element.249), channel_id=9, replica_groups=mesh['dp'=16,'fsdp'=2] {'dp','fsdp'}, dimensions={1}, use_global_device_ids=true | all-gather | bytes 38016 | tf_op jit(solution)/shard_map/all_gather | solution.py:52
  64.3 37.3 %all-gather.1 = bf16[1,768,24]{2,1,0:T(8,128)(2,1)S(1)} all-gather(bf16[1,24,24]{2,1,0:T(8,128)(2,1)S(1)} %get-tuple-element.250), channel_id=3, replica_groups=mesh['dp'=16,'fsdp'=2] {'dp','fsdp'}, dimensions={1}, use_global_device_ids=true | all-gather | bytes 38016 | tf_op jit(solution)/shard_map/all_gather | solution.py:52
  107.5 37.7 %all-reduce.3 = (bf16[3072]{0:T(1024)(128)(2,1)S(1)}, bf16[3072]{0:T(1024)(128)(2,1)S(1)}) all-reduce(bf16[3072]{0:T(1024)(128)(2,1)S(1)} %dynamic-update-slice, bf16[3072]{0:T(1024)(128)(2,1)S(1)} %dynamic-update-slice.1), channel_id=6, replica_groups=mesh['dp'=16,'fsdp'=2] {'dp','fsdp'}, use_global_device_ids=true, to_apply=%add | all-reduce | flops 6144 | bytes 24576
  148.9 9.4 %fusion.54 = bf16[1024,2304]{1,0:T(8,128)(2,1)} fusion(f32[1024,768]{1,0:T(8,128)S(1)} %convolution_multiply_fusion.2, f32[1024,768]{1,0:T(8,128)} %convolution_multiply_fusion.3, bf16[1024,768]{1,0:T(8,128)(2,1)} %bitcast.377, f32[2304]{0:T(1024)S(1)} %get-tuple-element.255, f32[2304]{0:T(1024)S(1)} %get-tuple-element.254, ...), kind=kOutput, calls=%fused_computation.111 | convolution fusion | flops 3635675136 | bytes 16140288 | tf_op jit(solution)/shard_map/dot_general | solution.py:30
  165.1 18.2 %while.44 = (s32[]{:T(128)}, bf16[2,512,768]{2,1,0:T(8,128)(2,1)S(1)}, f32[2,12,512]{2,1,0:T(8,128)S(1)}, bf16[2,512,2304]{1,2,0:T(8,128)(2,1)}, s32[]{:T(128)}) while((s32[]{:T(128)}, bf16[2,512,768]{2,1,0:T(8,128)(2,1)S(1)}, f32[2,12,512]{2,1,0:T(8,128)S(1)}, bf16[2,512,2304]{1,2,0:T(8,128)(2,1)}, s32[]{:T(128)}) %tuple.124), condition=%wide.region_3.4_spmd, body=%wide.region_0.3_spmd.sunk | while | flops 834004992 | bytes 48996424 | solution.py:152
  188.7 8.0 all-gather.25.cloned.1.call-done
  196.8 36.3 %fusion.42 = (f32[1024,3072]{1,0:T(8,128)}, f32[1024,3072]{1,0:T(8,128)}) fusion(f32[3072]{0:T(1024)S(1)} %convert_element_type.210, bf16[1,768,3072]{2,1,0:T(8,128)(2,1)} %all-gather.25.cloned.1.call-done, f32[1024,768]{1,0:T(8,128)S(1)} %get-tuple-element.259, f32[768]{0:T(1024)S(1)} %get-tuple-element.177, f32[768]{0:T(1024)S(1)} %get-tuple-element.178, ...), kind=kOutput, calls=%fused_computation.78 | convolution fusion | flops 5033951232 | bytes 33056768 | tf_op jit(solution)/shard_map/dot_general | solution.py:30
  233.0 29.0 %all-gather.27.cloned.1.call-done = bf16[1,3072,768]{2,1,0:T(8,128)(2,1)} async-done(((bf16[1,96,768]{2,1,0:T(8,128)(2,1)}), bf16[1,3072,768]{2,1,0:T(8,128)(2,1)}) %all-gather.27.cloned.1.call-update) | async-done | bytes 4718608 | tf_op jit(solution)/shard_map/all_gather | solution.py:51
  262.1 12.7 %fusion.236 = (f32[1024]{0:T(1024)S(1)}, f32[1024,768]{1,0:T(8,128)S(1)}) fusion(f32[768]{0:T(1024)S(1)} %copy-done.73, bf16[1,3072,768]{2,1,0:T(8,128)(2,1)} %all-gather.27.cloned.1.call-done, f32[1024,3072]{1,0:T(8,128)} %get-tuple-element.260, f32[1024,3072]{1,0:T(8,128)} %get-tuple-element.261, f32[3072]{0:T(1024)S(1)} %convert_element_type.210, ...), kind=kOutput, calls=%fused_computation.320 | convolution fusion | flops 4849925120 | bytes 36209664 | tf_op jit(solution)/shard_map/dot_general | solution.py:30
  281.1 42.6 %all-gather.29.cloned.1.call-done = bf16[1,768,2304]{2,1,0:T(8,128)(2,1)} async-done(((bf16[1,24,2304]{2,1,0:T(8,128)(2,1)}), bf16[1,768,2304]{2,1,0:T(8,128)(2,1)}) %all-gather.29.cloned.1.call-update) | async-done | bytes 3538960 | tf_op jit(solution)/shard_map/all_gather | solution.py:47
  323.7 8.5 fusion.55
  332.2 6.7 copy.70
  339.0 18.2 %while.45 = (s32[]{:T(128)}, bf16[2,512,768]{2,1,0:T(8,128)(2,1)S(1)}, f32[2,12,512]{2,1,0:T(8,128)S(1)}, bf16[2,512,2304]{1,2,0:T(8,128)(2,1)}, s32[]{:T(128)}) while((s32[]{:T(128)}, bf16[2,512,768]{2,1,0:T(8,128)(2,1)S(1)}, f32[2,12,512]{2,1,0:T(8,128)S(1)}, bf16[2,512,2304]{1,2,0:T(8,128)(2,1)}, s32[]{:T(128)}) %tuple.127), condition=%wide.region_11.12_spmd, body=%wide.region_8.11_spmd.sunk | while | flops 834004992 | bytes 48996424 | solution.py:152
  357.3 22.6 %all-gather.31.cloned.1.call-done = bf16[1,768,768]{2,1,0:T(8,128)(2,1)} async-done(((bf16[1,24,768]{2,1,0:T(8,128)(2,1)}), bf16[1,768,768]{2,1,0:T(8,128)(2,1)}) %all-gather.31.cloned.1.call-update) | async-done | bytes 1179664 | tf_op jit(solution)/shard_map/all_gather | solution.py:48
  384.9 60.5 %all-gather.33.cloned.1.call-done = bf16[1,768,3072]{2,1,0:T(8,128)(2,1)} async-done(((bf16[1,24,3072]{2,1,0:T(8,128)(2,1)}), bf16[1,768,3072]{2,1,0:T(8,128)(2,1)}) %all-gather.33.cloned.1.call-update) | async-done | bytes 4718608 | tf_op jit(solution)/shard_map/all_gather | solution.py:49
  445.4 36.8 %fusion.43 = (f32[1024,3072]{1,0:T(8,128)}, f32[1024,3072]{1,0:T(8,128)}) fusion(f32[3072]{0:T(1024)S(1)} %copy-done.66, bf16[1,768,3072]{2,1,0:T(8,128)(2,1)} %all-gather.33.cloned.1.call-done, f32[1024,768]{1,0:T(8,128)S(1)} %get-tuple-element.265, f32[768]{0:T(1024)S(1)} %copy-done.71, f32[768]{0:T(1024)S(1)} %copy-done.69, f32[1024]{0:T(1024)S(1)} %fusion.214, ...), kind=kOutput, calls=%fused_computation.79 | convolution fusion | flops 5033951232 | bytes 33056768 | tf_op jit(solution)/shard_map/dot_general | solution.py:30
  482.2 28.5 %all-gather.35.cloned.1.call-done = bf16[1,3072,768]{2,1,0:T(8,128)(2,1)} async-done(((bf16[1,96,768]{2,1,0:T(8,128)(2,1)}), bf16[1,3072,768]{2,1,0:T(8,128)(2,1)}) %all-gather.35.cloned.1.call-update) | async-done | bytes 4718608 | tf_op jit(solution)/shard_map/all_gather | solution.py:51
  510.8 12.6 %fusion.238 = (f32[1024]{0:T(1024)S(1)}, f32[1024,768]{1,0:T(8,128)S(1)}) fusion(f32[768]{0:T(1024)S(1)} %copy-done.70, bf16[1,3072,768]{2,1,0:T(8,128)(2,1)} %all-gather.35.cloned.1.call-done, f32[1024,3072]{1,0:T(8,128)} %get-tuple-element.266, f32[1024,3072]{1,0:T(8,128)} %get-tuple-element.267, f32[3072]{0:T(1024)S(1)} %copy-done.66, ...), kind=kOutput, calls=%fused_computation.322 | convolution fusion | flops 4849925120 | bytes 36209664 | tf_op jit(solution)/shard_map/dot_general | solution.py:30
  527.7 22.2 %multiply_reduce_fusion.6 = (f32[1024]{0:T(1024)S(1)}, f32[1024,768]{1,0:T(8,128)}) fusion(f32[1024,768]{1,0:T(8,128)S(1)} %get-tuple-element.265, f32[1024]{0:T(1024)S(1)} %broadcast_multiply_fusion.1, f32[768]{0:T(1024)S(1)} %copy-done.69, bf16[1,768,3072]{2,1,0:T(8,128)(2,1)} %all-gather.33.cloned.1.call-done, f32[1024,3072]{1,0:T(8,128)} %get-tuple-element.266, ...), kind=kOutput, calls=%fused_computation.150 | convolution fusion | flops 9717152768 | bytes 44067840 | tf_op jit(solution)/shard_map/dot_general | solution.py:34
  559.5 83.6 %while.46 = (s32[]{:T(128)}, bf16[2,512,2304]{2,1,0:T(8,128)(2,1)}, bf16[2,512,2304]{1,2,0:T(8,128)(2,1)}, f32[2,12,512]{2,1,0:T(8,128)S(1)}, bf16[2,512,768]{2,1,0:T(8,128)(2,1)}, /*index=5*/s32[]{:T(128)}) while((s32[]{:T(128)}, bf16[2,512,2304]{2,1,0:T(8,128)(2,1)}, bf16[2,512,2304]{1,2,0:T(8,128)(2,1)}, f32[2,12,512]{2,1,0:T(8,128)S(1)}, ...), condition=%wide.region_22.23_spmd, body=%wide.region_20.22_spmd.sunk | while | flops 2055333888 | bytes 168870656 | solution.py:216
  571.1 11.5 %multiply_reduce_fusion.18 = (f32[12,512]{1,0:T(8,128)S(1)}, f32[12,512,512]{1,2,0:T(8,128)}) fusion(f32[12,512,512]{1,2,0:T(8,128)} %fusion.291, f32[12,512]{1,0:T(8,128)S(1)} %dynamic-slice_bitcast_fusion.4, bf16[512,12,64]{0,2,1:T(8,128)(2,1)S(1)} %bitcast.347, bf16[512,3,12,64]{0,3,2,1:T(8,128)(2,1)S(1)} %bitcast.338), kind=kOutput, calls=%fused_computation.29.clone.1 | convolution fusion | flops 415229952 | bytes 26796032 | tf_op jit(solution)/shard_map/while/body/eval_jaxpr/qhd,khd->hqk/dot_general | solution.py:99
  582.7 6.9 multiply_convert_fusion.16
  612.7 11.5 %multiply_reduce_fusion.18 = (f32[12,512]{1,0:T(8,128)S(1)}, f32[12,512,512]{1,2,0:T(8,128)}) fusion(f32[12,512,512]{1,2,0:T(8,128)} %fusion.291, f32[12,512]{1,0:T(8,128)S(1)} %dynamic-slice_bitcast_fusion.4, bf16[512,12,64]{0,2,1:T(8,128)(2,1)S(1)} %bitcast.347, bf16[512,3,12,64]{0,3,2,1:T(8,128)(2,1)S(1)} %bitcast.338), kind=kOutput, calls=%fused_computation.29.clone.1 | convolution fusion | flops 415229952 | bytes 26796032 | tf_op jit(solution)/shard_map/while/body/eval_jaxpr/qhd,khd->hqk/dot_general | solution.py:99
  624.3 6.9 multiply_convert_fusion.16
  660.8 21.1 %multiply_reduce_fusion.4 = (f32[1024]{0:T(1024)S(1)}, f32[1024,768]{1,0:T(8,128)}) fusion(f32[1024,768]{1,0:T(8,128)S(1)} %copy-done.7, f32[1024]{0:T(1024)S(1)} %copy-done.46, f32[768]{0:T(1024)S(1)} %copy-done.68, bf16[1,768,3072]{2,1,0:T(8,128)(2,1)} %all-gather.25.cloned.1.call-done, f32[1024,3072]{1,0:T(8,128)} %get-tuple-element.260, ...), kind=kOutput, calls=%fused_computation.146 | convolution fusion | flops 9717152768 | bytes 44067840 | tf_op jit(solution)/shard_map/dot_general | solution.py:34
  691.6 82.6 %while.47 = (s32[]{:T(128)}, bf16[2,512,2304]{2,1,0:T(8,128)(2,1)}, bf16[2,512,2304]{1,2,0:T(8,128)(2,1)}, f32[2,12,512]{2,1,0:T(8,128)S(1)}, bf16[2,512,768]{2,1,0:T(8,128)(2,1)}, /*index=5*/s32[]{:T(128)}) while((s32[]{:T(128)}, bf16[2,512,2304]{2,1,0:T(8,128)(2,1)}, bf16[2,512,2304]{1,2,0:T(8,128)(2,1)}, f32[2,12,512]{2,1,0:T(8,128)S(1)}, ...), condition=%wide.region_29.30_spmd, body=%wide.region_27.29_spmd.sunk | while | flops 2055333888 | bytes 168477376 | solution.py:216
  702.5 11.5 %multiply_reduce_fusion.19 = (f32[12,512]{1,0:T(8,128)S(1)}, f32[12,512,512]{1,2,0:T(8,128)}) fusion(f32[12,512,512]{1,2,0:T(8,128)} %fusion.300, f32[12,512]{1,0:T(8,128)S(1)} %dynamic-slice_bitcast_fusion.5, bf16[512,12,64]{0,2,1:T(8,128)(2,1)S(1)} %bitcast.349, bf16[512,3,12,64]{0,3,2,1:T(8,128)(2,1)S(1)} %bitcast.342), kind=kOutput, calls=%fused_computation.53.clone.1 | convolution fusion | flops 415229952 | bytes 26796032 | tf_op jit(solution)/shard_map/while/body/eval_jaxpr/qhd,khd->hqk/dot_general | solution.py:99
  714.5 6.9 multiply_convert_fusion.17
  743.6 11.5 %multiply_reduce_fusion.19 = (f32[12,512]{1,0:T(8,128)S(1)}, f32[12,512,512]{1,2,0:T(8,128)}) fusion(f32[12,512,512]{1,2,0:T(8,128)} %fusion.300, f32[12,512]{1,0:T(8,128)S(1)} %dynamic-slice_bitcast_fusion.5, bf16[512,12,64]{0,2,1:T(8,128)(2,1)S(1)} %bitcast.349, bf16[512,3,12,64]{0,3,2,1:T(8,128)(2,1)S(1)} %bitcast.342), kind=kOutput, calls=%fused_computation.53.clone.1 | convolution fusion | flops 415229952 | bytes 26796032 | tf_op jit(solution)/shard_map/while/body/eval_jaxpr/qhd,khd->hqk/dot_general | solution.py:99
  755.7 6.9 multiply_convert_fusion.17
  782.9 6.9 fusion.87
  792.5 111.5 %all-reduce.6.cloned.1.call-done = (f32[1,8,768]{2,1,0:T(8,128)}, f32[1,8,768]{2,1,0:T(8,128)}, f32[1,8,768]{2,1,0:T(8,128)}, f32[1,8,768]{2,1,0:T(8,128)}) async-done(((f32[1,8,768]{2,1,0:T(8,128)}, f32[1,8,768]{2,1,0:T(8,128)}, f32[1,8,768]{2,1,0:T(8,128)}, f32[1,8,768]{2,1,0:T(8,128)}), (f32[1,8,768]{2,1,0:T(8,128)}, f32[1,8,768]{2,1,0:T(8,128)}, f32[1,8,768]{2,1,0:T(8,128)}, ...) | async-done | bytes 98320 | tf_op jit(solution)/shard_map/psum | solution.py:311
  (361 shorter events, 227.0 us)
Async XLA Ops:
  7.2 138.7 %copy-start = (bf16[2,80,768]{2,1,0:T(8,128)(2,1)S(1)}, bf16[2,80,768]{2,1,0:T(8,128)(2,1)}, u32[]{:S(2)}) copy-start(bf16[2,80,768]{2,1,0:T(8,128)(2,1)} %param.21) | copy-start | bytes 737284
  7.2 141.7 %all-gather.21.cloned.1.call-start = ((), (), s32[]{:S(2)}) async-start(), calls=%async_computation | async-start | bytes 3649536 | tf_op jit(solution)/shard_map/all_gather | solution.py:47
  9.0 174.3 %all-gather.23.cloned.1.call-start = ((), (), s32[]{:S(2)}) async-start(), calls=%async_computation.1 | async-start | bytes 1216512 | tf_op jit(solution)/shard_map/all_gather | solution.py:48
  10.5 186.3 %all-gather.25.cloned.1.call-start = ((), (), s32[]{:S(2)}) async-start(), calls=%async_computation.2 | async-start | bytes 4866048 | tf_op jit(solution)/shard_map/all_gather | solution.py:49
  12.3 91.1 %copy-start.40 = (f32[2,8,768]{2,1,0:T(8,128)S(1)}, f32[2,8,768]{2,1,0:T(8,128)}, u32[]{:S(2)}) copy-start(f32[2,8,768]{2,1,0:T(8,128)} %param.31) | copy-start | bytes 147460
  12.3 91.1 %copy-start.41 = (f32[2,8,768]{2,1,0:T(8,128)S(1)}, f32[2,8,768]{2,1,0:T(8,128)}, u32[]{:S(2)}) copy-start(f32[2,8,768]{2,1,0:T(8,128)} %param.30) | copy-start | bytes 147460
  12.3 91.2 %copy-start.19 = (bf16[2,512,768]{2,1,0:T(8,128)(2,1)S(1)}, bf16[2,512,768]{2,1,0:T(8,128)(2,1)}, u32[]{:S(2)}) copy-start(bf16[2,512,768]{2,1,0:T(8,128)(2,1)} %param.20) | copy-start | bytes 4718596
  12.3 249.8 %all-gather.27.cloned.1.call-start = ((), (), s32[]{:S(2)}) async-start(), calls=%async_computation.3 | async-start | bytes 4866048 | tf_op jit(solution)/shard_map/all_gather | solution.py:51
  14.2 309.5 %all-gather.29.cloned.1.call-start = ((), (), s32[]{:S(2)}) async-start(), calls=%async_computation.4 | async-start | bytes 3649536 | tf_op jit(solution)/shard_map/all_gather | solution.py:47
  14.8 365.1 %all-gather.31.cloned.1.call-start = ((), (), s32[]{:S(2)}) async-start(), calls=%async_computation.5 | async-start | bytes 1216512 | tf_op jit(solution)/shard_map/all_gather | solution.py:48
  15.4 430.0 %all-gather.33.cloned.1.call-start = ((), (), s32[]{:S(2)}) async-start(), calls=%async_computation.6 | async-start | bytes 4866048 | tf_op jit(solution)/shard_map/all_gather | solution.py:49
  16.1 494.7 %all-gather.35.cloned.1.call-start = ((), (), s32[]{:S(2)}) async-start(), calls=%async_computation.7 | async-start | bytes 4866048 | tf_op jit(solution)/shard_map/all_gather | solution.py:51
  16.9 887.1 %all-reduce.6.cloned.1.call-start = ((), (), s32[]{:S(2)}) async-start(), calls=%async_computation.8 | async-start | bytes 196608 | tf_op jit(solution)/shard_map/psum | solution.py:311
  103.4 158.7 %copy-start.67 = (f32[768]{0:T(1024)}, f32[768]{0:T(1024)S(1)}, u32[]{:S(2)}) copy-start(f32[768]{0:T(1024)S(1)} %get-tuple-element.178) | copy-start | bytes 9220
  145.2 116.8 %copy-start.64 = (f32[3072]{0:T(1024)}, f32[3072]{0:T(1024)S(1)}, u32[]{:S(2)}) copy-start(f32[3072]{0:T(1024)S(1)} %convert_element_type.210) | copy-start | bytes 36868
  188.2 73.9 %copy-start.6 = (f32[1024,768]{1,0:T(8,128)}, f32[1024,768]{1,0:T(8,128)S(1)}, u32[]{:S(2)}) copy-start(f32[1024,768]{1,0:T(8,128)S(1)} %get-tuple-element.259) | copy-start | bytes 9437188
  188.2 73.8 %copy-start.45 = (f32[1024]{0:T(1024)}, f32[1024]{0:T(1024)S(1)}, u32[]{:S(2)}) copy-start(f32[1024]{0:T(1024)S(1)} %broadcast_multiply_fusion.3) | copy-start | bytes 12292
  188.7 73.3 %copy-start.55 = (f32[1024]{0:T(1024)}, f32[1024]{0:T(1024)S(1)}, u32[]{:S(2)}) copy-start(f32[1024]{0:T(1024)S(1)} %fusion.212) | copy-start | bytes 12292
  196.8 65.3 %copy-start.73 = (f32[768]{0:T(1024)S(1)}, f32[768]{0:T(1024)}, u32[]{:S(2)}) copy-start(f32[768]{0:T(1024)} %get-tuple-element.176) | copy-start | bytes 9220
  274.8 105.1 %copy-start.30 = (f32[1024]{0:T(1024)}, f32[1024]{0:T(1024)S(1)}, u32[]{:S(2)}) copy-start(f32[1024]{0:T(1024)S(1)} %broadcast_multiply_fusion.2) | copy-start | bytes 12292
  275.3 104.5 %copy-start.47 = (f32[1024]{0:T(1024)}, f32[1024]{0:T(1024)S(1)}, u32[]{:S(2)}) copy-start(f32[1024]{0:T(1024)S(1)} %fusion.213) | copy-start | bytes 12292
  275.9 47.8 %copy-start.61 = (f32[2304]{0:T(1024)S(1)}, f32[2304]{0:T(1024)}, u32[]{:S(2)}) copy-start(f32[2304]{0:T(1024)} %get-tuple-element.253) | copy-start | bytes 27652
  276.5 55.7 %copy-start.28 = (bf16[1024,16]{0,1:T(8,128)(2,1)}, bf16[1024,16]{0,1:T(8,128)(2,1)S(1)}, u32[]{:S(2)}) copy-start(bf16[1024,16]{0,1:T(8,128)(2,1)S(1)} %convolution_convert_fusion.2) | copy-start | bytes 98308
  379.9 65.5 %copy-start.66 = (f32[3072]{0:T(1024)S(1)}, f32[3072]{0:T(1024)}, u32[]{:S(2)}) copy-start(f32[3072]{0:T(1024)} %convert_element_type.211) | copy-start | bytes 36868
  379.9 65.5 %copy-start.69 = (f32[768]{0:T(1024)S(1)}, f32[768]{0:T(1024)}, u32[]{:S(2)}) copy-start(f32[768]{0:T(1024)} %get-tuple-element.170) | copy-start | bytes 9220
  379.9 65.5 %copy-start.71 = (f32[768]{0:T(1024)S(1)}, f32[768]{0:T(1024)}, u32[]{:S(2)}) copy-start(f32[768]{0:T(1024)} %get-tuple-element.169) | copy-start | bytes 9220
  445.4 65.4 %copy-start.70 = (f32[768]{0:T(1024)S(1)}, f32[768]{0:T(1024)}, u32[]{:S(2)}) copy-start(f32[768]{0:T(1024)} %get-tuple-element.168) | copy-start | bytes 9220
  559.5 83.6 %copy-start.29 = (bf16[1024,16]{0,1:T(8,128)(2,1)S(1)}, bf16[1024,16]{0,1:T(8,128)(2,1)}, u32[]{:S(2)}) copy-start(bf16[1024,16]{0,1:T(8,128)(2,1)} %copy-done.28) | copy-start | bytes 98308
  559.5 88.5 %copy-start.34 = (bf16[2,8,768]{2,1,0:T(8,128)(2,1)S(1)}, bf16[2,8,768]{2,1,0:T(8,128)(2,1)}, u32[]{:S(2)}) copy-start(bf16[2,8,768]{2,1,0:T(8,128)(2,1)} %copy-done.32) | copy-start | bytes 73732
  691.6 82.6 %copy-start.27 = (bf16[1024,16]{0,1:T(8,128)(2,1)S(1)}, bf16[1024,16]{0,1:T(8,128)(2,1)}, u32[]{:S(2)}) copy-start(bf16[1024,16]{0,1:T(8,128)(2,1)} %copy-done.26) | copy-start | bytes 98308
  691.6 87.3 %copy-start.39 = (bf16[2,8,768]{2,1,0:T(8,128)(2,1)S(1)}, bf16[2,8,768]{2,1,0:T(8,128)(2,1)}, u32[]{:S(2)}) copy-start(bf16[2,8,768]{2,1,0:T(8,128)(2,1)} %copy-done.36) | copy-start | bytes 73732
  782.8 122.6 %copy-start.1 = (bf16[2,80,768]{2,1,0:T(8,128)(2,1)S(1)}, bf16[2,80,768]{2,1,0:T(8,128)(2,1)}, u32[]{:S(2)}) copy-start(bf16[2,80,768]{2,1,0:T(8,128)(2,1)} %param.21) | copy-start | bytes 737284
  (72 other events, 697.3 us)
Sparse Core Ops, SparseCore 0:
  11.5 63.4 all-gather.20
  78.5 52.6 all-gather.22
  134.1 62.6 all-gather.24
  199.5 62.4 all-gather.26
  264.8 58.8 all-gather.28
  327.0 52.8 all-gather.30
  382.8 62.5 all-gather.32
  448.3 62.4 all-gather.34
  782.9 121.0 all-reduce.5
where the time goes:
time: 919 us; the launch traced here: 912 us
  matrix products  330 us (36%)
  waiting for transfers between devices  305 us (33%)
  blocking collectives  119 us (13%)
  local copies, waits for them, and re-layouts  87.3 us (9%)
  other arithmetic  53.9 us (6%)
  between operations  15.3 us (2%)
    dot_general x14, matrix products, matrix_multiply(): return jnp.dot(left, right, preferred_element_type=jnp.float32)  133 us
    psum x1, waiting for transfers between devices, on_device(): lax.psum((query_gradient_total, value_gradient_total), ('dp', 'fsdp'))  112 us
    all_gather x2, blocking collectives, fetch_forward(): lax.all_gather(layer_small, ('dp', 'fsdp'), axis=0, tiled=True)  81.3 us
    dot_general x12, matrix products, transposed_multiply(): lax.dot_general(left, right, (((1,), (1,)), ((), ())), preferred_element_...  72.1 us
    all_gather x2, waiting for transfers between devices, fetch_forward(): lax.all_gather(layer_in, ('dp', 'fsdp'), axis=0, tiled=True)  68.5 us
    all_gather x2, waiting for transfers between devices, fetch_forward(): lax.all_gather(layer_out, ('dp', 'fsdp'), axis=0, tiled=True)  57.5 us
    dot_general x4, matrix products, attend_back(): jnp.einsum('qhd,khd->hqk', grad_view, value_matrix_rows, preferred_elemen...  46.1 us
    all_gather x2, waiting for transfers between devices, fetch_forward(): lax.all_gather(layer_qkv, ('dp', 'fsdp'), axis=0, tiled=True)  42.6 us
  transfers between devices with their start and end apart: 9, of which 7 were waited for; matrix products, arithmetic and copies ran while one was open for 21% of the time, Pallas kernels for 0%

commit v1 on v0

v1 whole, which is shorter than its diff:
```python
import functools

import jax
import jax.numpy as jnp
from jax import lax
from jax.experimental import pallas as pl
from jax.experimental.pallas import tpu as pltpu
from jax.sharding import PartitionSpec as P

D = 768
H = 12
HD = 64
FF = 3072
RANK = 8
LAYERS = 2
LEN = 512
MAXM = 80
EPS = 1e-05
SCALE = 0.125
BF = jnp.bfloat16
F32 = jnp.float32
AXES = ("dp", "fsdp")
INV_SQRT2 = 0.7071067811865476
INV_SQRT2PI = 0.3989422804014327
ROWS = 256


def nn(a, b):
    return lax.dot_general(a, b, (((1,), (0,)), ((), ())), preferred_element_type=F32)


def nt(a, b):
    return lax.dot_general(a, b, (((1,), (1,)), ((), ())), preferred_element_type=F32)


def tn(a, b):
    return lax.dot_general(a, b, (((0,), (0,)), ((), ())), preferred_element_type=F32)


def flat(ref):
    v = ref[...]
    return v.reshape(v.shape[0] * v.shape[1], v.shape[2])


def norm_stats(r):
    mean = jnp.mean(r, axis=-1, keepdims=True)
    c = r - mean
    rstd = lax.rsqrt(jnp.mean(c * c, axis=-1, keepdims=True) + EPS)
    return c * rstd, rstd


def norm_back(e, n, rstd, gain):
    eg = e * gain
    a = jnp.mean(eg, axis=-1, keepdims=True)
    b = jnp.mean(eg * n, axis=-1, keepdims=True)
    return rstd * (eg - a - n * b)


def params(n_steps=1):
    return pltpu.CompilerParams(
        dimension_semantics=("arbitrary",) * n_steps, vmem_limit_bytes=60 << 20
    )


def whole(shape):
    zero = (0,) * len(shape)
    return pl.BlockSpec(shape, lambda *_: zero)


def sds(shape, dtype):
    return jax.ShapeDtypeStruct(shape, dtype)


def unit_spec(packed, index):
    nb = packed.shape[0]
    rb = packed.shape[1] // 12
    return pl.BlockSpec((nb, rb, D), lambda *g: (0, index(*g), 0))


def out_spec(packed, index):
    nb = packed.shape[0]
    rb = packed.shape[1] // 12
    if nb % 4 == 0:
        return pl.BlockSpec((nb // 4, 4 * rb, D), lambda *g: (index(*g), 2, 0))
    return pl.BlockSpec((nb, rb, D), lambda *g: (0, 8 + index(*g), 0))


def qkv_kernel(x_ref, w_ref, a_ref, b_ref, bias_ref, o_ref, u_ref, wp_ref):
    j = pl.program_id(0)
    a = a_ref[...]
    wp_ref[...] = (flat(w_ref).astype(F32) + nn(a, b_ref[0])).astype(BF)
    t = x_ref.shape[0]
    for r in range(0, t, ROWS):
        x = x_ref[r : r + ROWS, :]
        o_ref[r : r + ROWS, :] = (nn(x, wp_ref[...]) + bias_ref[0]).astype(BF)

    @pl.when(j == 0)
    def _():
        u_ref[...] = nn(x_ref[...], a).astype(BF)


def qkv_call(x, packed, down, up3, bias3):
    t = x.shape[0]
    return pl.pallas_call(
        qkv_kernel,
        grid=(3,),
        in_specs=[
            whole((t, D)),
            unit_spec(packed, lambda j: j),
            whole(down.shape),
            pl.BlockSpec((1, 2 * RANK, D), lambda j: (j, 0, 0)),
            pl.BlockSpec((1, 1, D), lambda j: (j, 0, 0)),
        ],
        out_specs=[
            pl.BlockSpec((t, D), lambda j: (0, j)),
            whole((t, 2 * RANK)),
            pl.BlockSpec((D, D), lambda j: (0, j)),
        ],
        out_shape=[sds((t, 3 * D), BF), sds((t, 2 * RANK), BF), sds((D, 3 * D), BF)],
        compiler_params=params(),
        name="qkv",
    )(x, packed, down, up3, bias3)


PAIRS = H // 2


def head_spec(offset):
    return pl.BlockSpec((LEN, 2 * HD), lambda s, h: (s, offset * PAIRS + h))


def attn_kernel(q_ref, k_ref, v_ref, c_ref, z_ref):
    low = lax.broadcasted_iota(jnp.int32, (LEN, 2 * HD), 1) < HD
    q = q_ref[...] * jnp.asarray(SCALE, BF)
    k = k_ref[...]
    v = v_ref[...]
    ctx = []
    zs = []
    for h in range(2):
        mine = low if h == 0 else jnp.logical_not(low)
        s = nt(jnp.where(mine, q, jnp.zeros_like(q)), k)
        m = jnp.max(s, axis=-1, keepdims=True)
        p = jnp.exp(s - m).astype(BF)
        o = nn(p, jnp.where(mine, v, jnp.ones_like(v)))
        total = pltpu.roll(o, HD, 1)
        ctx.append(o / total)
        zs.append(m + jnp.log(total))
    c_ref[...] = jnp.where(low, ctx[0], ctx[1]).astype(BF)
    z_ref[...] = jnp.where(low, zs[0], zs[1])


def attn_call(qkv):
    t = qkv.shape[0]
    return pl.pallas_call(
        attn_kernel,
        grid=(t // LEN, PAIRS),
        in_specs=[head_spec(0), head_spec(1), head_spec(2)],
        out_specs=[head_spec(0), head_spec(0)],
        out_shape=[sds((t, D), BF), sds((t, D), F32)],
        compiler_params=params(2),
        name="attn_fwd",
    )(qkv, qkv, qkv)


def ffn_kernel(keep, h_ref, c_ref, wo_ref, win_ref, wout_ref, par_ref, fb_ref, *rest):
    if keep:
        hb_ref, n1_ref, s1_ref, n2_ref, s2_ref, ho_ref, gp_ref, h1_ref, acc_ref = rest
    else:
        hb_ref, n1_ref, s1_ref, n2_ref, s2_ref, h1_ref, acc_ref = rest
    j = pl.program_id(0)
    t = h_ref.shape[0]

    @pl.when(j == 0)
    def _():
        wo = flat(wo_ref)
        for r in range(0, t, ROWS):
            w = slice(r, r + ROWS)
            r1 = h_ref[w, :].astype(F32) + (nn(c_ref[w, :], wo) + par_ref[2:3, :])
            n1, s1 = norm_stats(r1)
            n1_ref[w, :] = n1.astype(BF)
            s1_ref[w, :] = s1
            h1 = n1 * par_ref[3:4, :] + par_ref[4:5, :]
            h1_ref[w, :] = h1.astype(BF)
            acc_ref[w, :] = h1 + par_ref[5:6, :]

    win = flat(win_ref)
    wout = flat(wout_ref)
    for r in range(0, t, ROWS):
        w = slice(r, r + ROWS)
        f = nn(h1_ref[w, :], win) + fb_ref[...]
        cdf = 0.5 + 0.5 * lax.erf(f * INV_SQRT2)
        act = (f * cdf).astype(BF)
        if keep:
            gp_ref[w, :] = (cdf + f * (INV_SQRT2PI * jnp.exp(-0.5 * (f * f)))).astype(BF)
        acc_ref[w, :] += nn(act, wout)

    @pl.when(j == 3)
    def _():
        for r in range(0, t, ROWS):
            w = slice(r, r + ROWS)
            n2, s2 = norm_stats(acc_ref[w, :])
            n2_ref[w, :] = n2.astype(BF)
            s2_ref[w, :] = s2
            h = n2 * par_ref[6:7, :] + par_ref[7:8, :]
            hb_ref[w, :] = h.astype(BF)
            if keep:
                ho_ref[w, :] = h


def ffn_call(h, ctx, packed, par, fb, keep):
    t = h.shape[0]
    out_specs = [whole((t, D)), whole((t, D)), whole((t, 1)), whole((t, D)), whole((t, 1))]
    out_shape = [sds((t, D), BF), sds((t, D), BF), sds((t, 1), F32), sds((t, D), BF), sds((t, 1), F32)]
    if keep:
        out_specs += [whole((t, D)), pl.BlockSpec((t, D), lambda j: (0, j))]
        out_shape += [sds((t, D), F32), sds((t, FF), BF)]
    return pl.pallas_call(
        functools.partial(ffn_kernel, keep),
        grid=(4,),
        in_specs=[
            whole((t, D)),
            whole((t, D)),
            unit_spec(packed, lambda j: 3),
            unit_spec(packed, lambda j: 4 + j),
            out_spec(packed, lambda j: j),
            whole(par.shape),
            pl.BlockSpec((1, D), lambda j: (0, j)),
        ],
        out_specs=out_specs,
        out_shape=out_shape,
        scratch_shapes=[pltpu.VMEM((t, D), BF), pltpu.VMEM((t, D), F32)],
        compiler_params=params(),
        name="ffn_fwd",
    )(h, ctx, packed, packed, packed, par, fb)


def pick(pos_ref, s, dtype):
    column = pos_ref[s * MAXM : (s + 1) * MAXM, :]
    return (lax.broadcasted_iota(jnp.int32, (MAXM, LEN), 1) == column).astype(dtype)


def ffn_pick_kernel(
    seqs, cnt_ref, cot_ref, pos_ref, n1_ref, s1_ref, n2_ref, s2_ref, wo_ref, win_ref, wout_ref, par_ref, fb_ref,
    dr1_ref, dctx_ref, h1_ref, d2_ref, n1s_ref, s1s_ref, acc_ref,
):
    j = pl.program_id(0)

    @pl.when(j == 0)
    def _():
        for s in range(seqs):
            w = slice(s * LEN, (s + 1) * LEN)
            m = slice(s * MAXM, (s + 1) * MAXM)
            onehot = pick(pos_ref, s, BF)
            onehot_f = pick(pos_ref, s, F32)

            def take(v):
                return lax.dot_general(
                    onehot_f, v, (((1,), (0,)), ((), ())),
                    precision=lax.Precision.HIGHEST, preferred_element_type=F32,
                )

            n1 = nn(onehot, n1_ref[w, :])
            n2 = nn(onehot, n2_ref[w, :])
            live = lax.broadcasted_iota(jnp.int32, (MAXM, D), 0) < cnt_ref[s]
            e = jnp.where(live, cot_ref[m, :].astype(F32), 0.0)
            d2 = norm_back(e, n2, take(s2_ref[w, :]), par_ref[6:7, :])
            n1s_ref[m, :] = n1
            s1s_ref[m, :] = take(s1_ref[w, :])
            h1_ref[m, :] = (n1 * par_ref[3:4, :] + par_ref[4:5, :]).astype(BF)
            d2_ref[m, :] = d2.astype(BF)
            acc_ref[m, :] = d2

    win = flat(win_ref)
    f = nn(h1_ref[...], win) + fb_ref[...]
    cdf = 0.5 + 0.5 * lax.erf(f * INV_SQRT2)
    gp = cdf + f * (INV_SQRT2PI * jnp.exp(-0.5 * (f * f)))
    df = (nt(d2_ref[...], flat(wout_ref)) * gp).astype(BF)
    acc_ref[...] += nt(df, win)

    @pl.when(j == 3)
    def _():
        d1 = norm_back(acc_ref[...], n1s_ref[...], s1s_ref[...], par_ref[3:4, :])
        dr1_ref[...] = d1
        dctx_ref[...] = nt(d1.astype(BF), flat(wo_ref)).astype(BF)


def ffn_pick_call(cot, pos, counts, n1, s1, n2, s2, packed, par, fb):
    t = n1.shape[0]
    seqs = t // LEN
    m = seqs * MAXM
    return pl.pallas_call(
        functools.partial(ffn_pick_kernel, seqs),
        grid=(4,),
        in_specs=[
            pl.BlockSpec(memory_space=pltpu.SMEM),
            whole((m, D)),
            whole((m, 1)),
            whole((t, D)),
            whole((t, 1)),
            whole((t, D)),
            whole((t, 1)),
            unit_spec(packed, lambda j: 3),
            unit_spec(packed, lambda j: 4 + j),
            out_spec(packed, lambda j: j),
            whole(par.shape),
            pl.BlockSpec((1, D), lambda j: (0, j)),
        ],
        out_specs=[whole((m, D)), whole((m, D))],
        out_shape=[sds((m, D), F32), sds((m, D), BF)],
        scratch_shapes=[
            pltpu.VMEM((m, D), BF),
            pltpu.VMEM((m, D), BF),
            pltpu.VMEM((m, D), F32),
            pltpu.VMEM((m, 1), F32),
            pltpu.VMEM((m, D), F32),
        ],
        compiler_params=params(),
        name="ffn_bwd_rows",
    )(counts, cot, pos, n1, s1, n2, s2, packed, packed, packed, par, fb)


def attn_pick_kernel(q_ref, k_ref, v_ref, g_ref, pos_ref, u_ref, dq_ref, dk_ref, dv_ref, gq_ref, gv_ref):
    low = lax.broadcasted_iota(jnp.int32, (LEN, 2 * HD), 1) < HD
    low_m = lax.broadcasted_iota(jnp.int32, (MAXM, 2 * HD), 1) < HD
    onehot = pick(pos_ref, 0, BF)
    qs = nn(onehot, q_ref[...]).astype(BF)
    qsc = qs * jnp.asarray(SCALE, BF)
    us = nn(onehot, u_ref[...]).astype(BF)
    k = k_ref[...]
    v = v_ref[...]
    g = g_ref[...]
    dqs, dks, dvs = [], [], []
    for h in range(2):
        mine = low_m if h == 0 else jnp.logical_not(low_m)
        s = nt(jnp.where(mine, qsc, jnp.zeros_like(qsc)), k)
        p = jnp.exp(s - jnp.max(s, axis=-1, keepdims=True))
        p = p * (1.0 / jnp.sum(p, axis=-1, keepdims=True))
        dp = nt(jnp.where(mine, g, jnp.zeros_like(g)), v)
        ds = (p * (dp - jnp.sum(p * dp, axis=-1, keepdims=True))).astype(BF)
        dqs.append(nn(ds, k))
        dks.append(tn(ds, qs))
        dvs.append(tn(p.astype(BF), g))
    dq = (jnp.where(low_m, dqs[0], dqs[1]) * SCALE).astype(BF)
    dv = jnp.where(low, dvs[0], dvs[1]).astype(BF)
    dq_ref[...] = dq
    dk_ref[...] = (jnp.where(low, dks[0], dks[1]) * SCALE).astype(BF)
    dv_ref[...] = dv
    gq_ref[0] = 2.0 * tn(us, dq)
    gv_ref[0] = 2.0 * tn(u_ref[...], dv)


def attn_pick_call(qkv, g, pos, u):
    t = qkv.shape[0]
    seqs = t // LEN
    grads = pl.BlockSpec((1, 2 * RANK, 2 * HD), lambda s, h: (s, 0, h))
    rows = pl.BlockSpec((MAXM, 2 * HD), lambda s, h: (s, h))
    return pl.pallas_call(
        attn_pick_kernel,
        grid=(seqs, PAIRS),
        in_specs=[
            head_spec(0),
            head_spec(1),
            head_spec(2),
            rows,
            pl.BlockSpec((MAXM, 1), lambda s, h: (s, 0)),
            pl.BlockSpec((LEN, 2 * RANK), lambda s, h: (s, 0)),
        ],
        out_specs=[rows, head_spec(0), head_spec(0), grads, grads],
        out_shape=[
            sds((seqs * MAXM, D), BF),
            sds((t, D), BF),
            sds((t, D), BF),
            sds((seqs, 2 * RANK, D), F32),
            sds((seqs, 2 * RANK, D), F32),
        ],
        compiler_params=params(2),
        name="attn_bwd_rows",
    )(qkv, qkv, qkv, g, pos, u)


def dh_pick_kernel(dr1_ref, dq_ref, dk_ref, dv_ref, pos_ref, w_ref, o_ref):
    rows = dr1_ref[...] + nt(dq_ref[...], w_ref[:, 0:D])
    high = rows.astype(BF)
    rest = (rows - high.astype(F32)).astype(BF)
    onehot = (lax.broadcasted_iota(jnp.int32, (LEN, MAXM), 0) == pos_ref[0]).astype(BF)
    o_ref[...] = (
        nt(dk_ref[...], w_ref[:, D : 2 * D])
        + nt(dv_ref[...], w_ref[:, 2 * D : 3 * D])
        + nn(onehot, high)
        + nn(onehot, rest)
    )


def dh_pick_call(dr1, dq, dk, dv, pos_row, wp):
    t = dk.shape[0]
    rows = pl.BlockSpec((MAXM, D), lambda s: (s, 0))
    block = pl.BlockSpec((LEN, D), lambda s: (s, 0))
    return pl.pallas_call(
        dh_pick_kernel,
        grid=(t // LEN,),
        in_specs=[rows, rows, block, block, pl.BlockSpec((1, 1, MAXM), lambda s: (s, 0, 0)), whole((D, 3 * D))],
        out_specs=block,
        out_shape=sds((t, D), F32),
        compiler_params=params(),
        name="dh_rows",
    )(dr1, dq, dk, dv, pos_row, wp)


def ffn_back_kernel(e_ref, n1_ref, s1_ref, n2_ref, s2_ref, gp_ref, wo_ref, win_ref, wout_ref, par_ref,
                    dr1_ref, dctx_ref, d2_ref, acc_ref):
    j = pl.program_id(0)
    t = e_ref.shape[0]

    @pl.when(j == 0)
    def _():
        for r in range(0, t, ROWS):
            w = slice(r, r + ROWS)
            d2 = norm_back(e_ref[w, :], n2_ref[w, :].astype(F32), s2_ref[w, :], par_ref[6:7, :])
            d2_ref[w, :] = d2.astype(BF)
            acc_ref[w, :] = d2

    win = flat(win_ref)
    wout = flat(wout_ref)
    for r in range(0, t, ROWS):
        w = slice(r, r + ROWS)
        df = (nt(d2_ref[w, :], wout) * gp_ref[w, :].astype(F32)).astype(BF)
        acc_ref[w, :] += nt(df, win)

    @pl.when(j == 3)
    def _():
        wo = flat(wo_ref)
        for r in range(0, t, ROWS):
            w = slice(r, r + ROWS)
            d1 = norm_back(acc_ref[w, :], n1_ref[w, :].astype(F32), s1_ref[w, :], par_ref[3:4, :])
            dr1_ref[w, :] = d1
            dctx_ref[w, :] = nt(d1.astype(BF), wo).astype(BF)


def ffn_back_call(e, n1, s1, n2, s2, gp, packed, par):
    t = e.shape[0]
    return pl.pallas_call(
        ffn_back_kernel,
        grid=(4,),
        in_specs=[
            whole((t, D)),
            whole((t, D)),
            whole((t, 1)),
            whole((t, D)),
            whole((t, 1)),
            pl.BlockSpec((t, D), lambda j: (0, j)),
            unit_spec(packed, lambda j: 3),
            unit_spec(packed, lambda j: 4 + j),
            out_spec(packed, lambda j: j),
            whole(par.shape),
        ],
        out_specs=[whole((t, D)), whole((t, D))],
        out_shape=[sds((t, D), F32), sds((t, D), BF)],
        scratch_shapes=[pltpu.VMEM((t, D), BF), pltpu.VMEM((t, D), F32)],
        compiler_params=params(),
        name="ffn_bwd",
    )(e, n1, s1, n2, s2, gp, packed, packed, packed, par)


def attn_back_kernel(q_ref, k_ref, v_ref, g_ref, z_ref, u_ref, dq_ref, dk_ref, dv_ref, gq_ref, gv_ref):
    low = lax.broadcasted_iota(jnp.int32, (LEN, 2 * HD), 1) < HD
    q = q_ref[...]
    qsc = q * jnp.asarray(SCALE, BF)
    k = k_ref[...]
    v = v_ref[...]
    g = g_ref[...]
    zt = z_ref[...].T
    kt = k.T
    dqs, dks, dvs = [], [], []
    for h in range(2):
        mine = low if h == 0 else jnp.logical_not(low)
        st = nt(k, jnp.where(mine, qsc, jnp.zeros_like(q)))
        pt = jnp.exp(st - zt[h * HD : h * HD + 1, :])
        dpt = nt(v, jnp.where(mine, g, jnp.zeros_like(g)))
        ds = (pt * (dpt - jnp.sum(pt * dpt, axis=0, keepdims=True))).astype(BF)
        dvs.append(nn(pt.astype(BF), g))
        dks.append(nn(ds, q))
        dqs.append(nn(kt[h * HD : (h + 1) * HD, :], ds))
    dq = (jnp.concatenate(dqs, axis=0).T * SCALE).astype(BF)
    dv = jnp.where(low, dvs[0], dvs[1]).astype(BF)
    dq_ref[...] = dq
    dk_ref[...] = (jnp.where(low, dks[0], dks[1]) * SCALE).astype(BF)
    dv_ref[...] = dv
    gq_ref[0] = 2.0 * tn(u_ref[...], dq)
    gv_ref[0] = 2.0 * tn(u_ref[...], dv)


def attn_back_call(qkv, g, z, u):
    t = qkv.shape[0]
    seqs = t // LEN
    grads = pl.BlockSpec((1, 2 * RANK, 2 * HD), lambda s, h: (s, 0, h))
    return pl.pallas_call(
        attn_back_kernel,
        grid=(seqs, PAIRS),
        in_specs=[
            head_spec(0),
            head_spec(1),
            head_spec(2),
            head_spec(0),
            head_spec(0),
            pl.BlockSpec((LEN, 2 * RANK), lambda s, h: (s, 0)),
        ],
        out_specs=[head_spec(0), head_spec(0), head_spec(0), grads, grads],
        out_shape=[sds((t, D), BF)] * 3 + [sds((seqs, 2 * RANK, D), F32)] * 2,
        compiler_params=params(2),
        name="attn_bwd",
    )(qkv, qkv, qkv, g, z, u)


def dh_kernel(dr1_ref, dq_ref, dk_ref, dv_ref, w_ref, o_ref):
    o_ref[...] = (
        dr1_ref[...]
        + nt(dq_ref[...], w_ref[:, 0:D])
        + nt(dk_ref[...], w_ref[:, D : 2 * D])
        + nt(dv_ref[...], w_ref[:, 2 * D : 3 * D])
    )


def dh_call(dr1, dq, dk, dv, wp):
    t = dk.shape[0]
    block = pl.BlockSpec((ROWS, D), lambda i: (i, 0))
    return pl.pallas_call(
        dh_kernel,
        grid=(t // ROWS,),
        in_specs=[block, block, block, block, whole((D, 3 * D))],
        out_specs=block,
        out_shape=sds((t, D), F32),
        compiler_params=params(),
        name="dh",
    )(dr1, dq, dk, dv, wp)


def network(tokens, cotangent, positions, counts, packed, smalls, biases, query_up, value_up):
    seqs = tokens.shape[0]
    x = tokens.reshape(seqs * LEN, D)
    pos_col = positions.reshape(seqs * MAXM, 1)
    pos_row = positions.reshape(seqs, 1, MAXM)
    cot = cotangent.reshape(seqs * MAXM, D)
    h = x
    saved = []
    for layer in range(LAYERS):
        small = smalls[layer]
        par = small.astype(F32).T
        down = small[:, 8 : 8 + 2 * RANK]
        zero = jnp.zeros((RANK, D), BF)
        up3 = jnp.stack(
            [
                jnp.concatenate([2.0 * query_up[layer].astype(BF), zero]),
                jnp.concatenate([zero, zero]),
                jnp.concatenate([zero, 2.0 * value_up[layer].astype(BF)]),
            ]
        )
        bias3 = jnp.stack([par[0:1], jnp.zeros((1, D), F32), par[1:2]])
        keep = layer < LAYERS - 1
        qkv, u, wp = qkv_call(x, packed[layer], down, up3, bias3)
        ctx, z = attn_call(qkv)
        outs = ffn_call(h, ctx, packed[layer], par, biases[layer], keep)
        x, n1, s1, n2, s2 = outs[:5]
        gp = None
        if keep:
            h, gp = outs[5:]
        saved.append((qkv, u, wp, z, n1, s1, n2, s2, gp, par))
    activations = x.reshape(tokens.shape)

    grads = [None] * LAYERS
    qkv, u, wp, z, n1, s1, n2, s2, gp, par = saved[-1]
    dr1, dctx = ffn_pick_call(
        cot, pos_col, counts, n1, s1, n2, s2, packed[-1], par, biases[-1]
    )
    dq, dk, dv, gq, gv = attn_pick_call(qkv, dctx, pos_col, u)
    grads[-1] = (gq, gv)
    e = dh_pick_call(dr1, dq, dk, dv, pos_row, wp)
    for layer in reversed(range(LAYERS - 1)):
        qkv, u, wp, z, n1, s1, n2, s2, gp, par = saved[layer]
        dr1, dctx = ffn_back_call(e, n1, s1, n2, s2, gp, packed[layer], par)
        dq, dk, dv, gq, gv = attn_back_call(qkv, dctx, z, u)
        grads[layer] = (gq, gv)
        e = dh_call(dr1, dq, dk, dv, wp)
    out = []
    for gq, gv in grads:
        out.append(
            jnp.concatenate([jnp.sum(gq, 0)[:RANK], jnp.sum(gv, 0)[RANK:]])
        )
    return activations, e.reshape(tokens.shape), out


def column_blocks(w, n):
    return [w[:, i * D : (i + 1) * D] for i in range(n)]


def on_device(
    tokens, cotangent, positions, counts, w_qkv, w_o, w_in, b_in, w_out, small, query_up, value_up
):
    packed, smalls, biases = [], [], []
    for layer in range(LAYERS):
        shard = jnp.concatenate(
            column_blocks(w_qkv[layer], 3) + [w_o[layer]] + column_blocks(w_in[layer], 4) + [w_out[layer]]
        )
        rb = w_o.shape[1]
        if rb % 8 == 0:
            packed.append(lax.all_gather(shard, AXES, axis=0, tiled=False))
        else:
            g = lax.all_gather(shard, AXES, axis=0, tiled=False)
            units = [g[:, i * rb : (i + 1) * rb].reshape(1, D, D) for i in range(8)]
            units.append(g[:, 8 * rb :].reshape(1, FF, D))
            packed.append(jnp.concatenate(units, axis=1))
    tiny = jnp.concatenate(
        [small.reshape(-1), b_in.reshape(-1)]
    )
    tiny = lax.all_gather(tiny, AXES, axis=0, tiled=False)
    n = tiny.shape[0]
    cut = small.size
    sm = tiny[:, :cut].reshape(n, LAYERS, -1, small.shape[2])
    bi = tiny[:, cut:].reshape(n, LAYERS, -1)
    for layer in range(LAYERS):
        smalls.append(sm[:, layer].reshape(D, small.shape[2]))
        biases.append(bi[:, layer].reshape(1, FF).astype(F32))
    activations, d_tokens, grads = network(
        tokens, cotangent, positions, counts, packed, smalls, biases, query_up, value_up
    )
    g = lax.psum(jnp.stack(grads), AXES)
    return activations, d_tokens, g[:, :RANK], g[:, RANK:]


def solution(mesh):
    both = P(AXES, None, None)
    mid = P(None, AXES, None)
    in_specs = (both, both, P(AXES, None), P(AXES), mid, mid, mid, P(None, AXES), mid, mid, P(), P())
    out_specs = (both, both, P(), P())
    return jax.shard_map(on_device, mesh=mesh, in_specs=in_specs, out_specs=out_specs, check_vma=False)
```

time: 919 us -> 615 us (0.67)
  matrix products: 330 us -> 0 us
  Pallas kernels: 0 us -> 192 us
  blocking collectives: 119 us -> 0 us
  waiting for transfers between devices: 305 us -> 390 us
  local copies, waits for them, and re-layouts: 87.3 us -> 12.8 us
  other arithmetic: 53.9 us -> 4.08 us
    dot_general x59 -> x0, matrix products: 330 us -> none  [the longest x14 133 us: matrix_multiply(): return jnp.dot(left, right, preferred_element_type=jnp.float32)]
    pallas_call x0 -> x12, Pallas kernels: none -> 192 us  [the longest x2 43.7 us: ffn_call(): pl.pallas_call(functools.partial(ffn_kernel, keep), grid=(4,), in_specs=[...]
    unnamed x9 -> x5, waiting for transfers between devices: 2.55 us -> 122 us
    all_gather x2 -> x0, blocking collectives: 81.3 us -> none  [fetch_forward(): lax.all_gather(layer_small, ('dp', 'fsdp'), axis=0, tiled=True)]
    unnamed x1 -> x0, blocking collectives: 37.7 us -> none
    all_gather x8 -> x2, waiting for transfers between devices: 191 us -> 159 us  [on_device(): packed.append(lax.all_gather(shard, AXES, axis=0, tiled=False))]
    convert_element_type x9 -> x1, other arithmetic: 28.7 us -> 0.09 us  [on_device(): biases.append(bi[:, layer].reshape(1, FF).astype(F32))]
    dynamic_update_slice x16 -> x0, local copies, waits for them, and re-layouts: 24.6 us -> none  [the longest x8 23.2 us: layer_backward_pass(): lax.map(attend_back, (packed_projection.reshape(-1, LEN, 3 * MODEL_WIDTH)...]
  transfers between devices with their start and end apart: 9 -> 4, of which waited for: 7 -> 4; matrix products, arithmetic and copies ran while one was open for 21% -> 2% of each run, Pallas kernels for 0% -> 9%
where the time goes in v1:
time: 615 us; the launch traced here: 614 us
  waiting for transfers between devices  390 us (63%)
  Pallas kernels  192 us (31%)
  between operations  14.2 us (2%)
  local copies, waits for them, and re-layouts  12.8 us (2%)
    all_gather x2, waiting for transfers between devices, on_device(): packed.append(lax.all_gather(shard, AXES, axis=0, tiled=False))  159 us
    unnamed x5, waiting for transfers between devices  122 us
    psum x1, waiting for transfers between devices, on_device(): g = lax.psum(jnp.stack(grads), AXES)  110 us
    pallas_call x2, Pallas kernels, ffn_call(): pl.pallas_call(functools.partial(ffn_kernel, keep), grid=(4,), in_specs=[...  43.7 us
    pallas_call x2, Pallas kernels, attn_call(): pl.pallas_call(attn_kernel, grid=(t // LEN, PAIRS), in_specs=[head_spec(0...  32 us
    pallas_call x1, Pallas kernels, attn_back_call(): pl.pallas_call(attn_back_kernel, grid=(seqs, PAIRS), in_specs=[head_spec(...  26.7 us
    pallas_call x1, Pallas kernels, ffn_back_call(): pl.pallas_call(ffn_back_kernel, grid=(4,), in_specs=[whole((t, D)), whole...  21.8 us
    pallas_call x1, Pallas kernels, attn_pick_call(): pl.pallas_call(attn_pick_kernel, grid=(seqs, PAIRS), in_specs=[head_spec(...  20 us
  transfers between devices with their start and end apart: 4, of which 4 were waited for; matrix products, arithmetic and copies ran while one was open for 2% of the time, Pallas kernels for 9%

profile of v1, /device:TPU:0, one launch (start us, length us, event | category | flops | bytes accessed | tf_op | source)
XLA Modules:
  0.0 613.6 jit_solution(15930499096879592684)
XLA Ops:
  7.2 0.8 reshape.79
  8.1 0.7 reshape.80
  9.9 1.0 slice_bitcast_fusion.2
  10.9 1.0 slice_bitcast_fusion
  12.2 0.7 copy-done.3
  13.8 0.8 reshape.95.pos_ref
  14.7 0.8 pad_maximum_fusion.2
  15.5 120.8 %all-reduce.10.cloned.1.call-done = bf16[43008]{0:T(1024)(128)(2,1)} async-done(((bf16[43008]{0:T(1024)(128)(2,1)}), bf16[43008]{0:T(1024)(128)(2,1)}) %all-reduce.10.cloned.1.call-update) | async-done | bytes 86032
  136.3 1.0 reshape.91
  138.1 0.8 slice.189.a_ref
  139.0 0.8 slice.204.a_ref
  140.0 0.7 reshape.88.fb_ref
  140.7 0.7 reshape.89.fb_ref
  141.4 0.7 pad_maximum_fusion.4
  142.1 102.9 %all-gather.6.cloned.1.call-done = bf16[9216,768]{1,0:T(8,128)(2,1)} async-done(((bf16[288,768]{1,0:T(8,128)(2,1)}), bf16[9216,768]{1,0:T(8,128)(2,1)}) %all-gather.6.cloned.1.call-update) | async-done | bytes 14155792 | tf_op jit(solution)/shard_map/all_gather | solution.py:605
  245.0 9.5 %qkv.2 = (bf16[1024,2304]{1,0:T(8,128)(2,1)}, bf16[1024,16]{1,0:T(8,128)(2,1)}, bf16[768,2304]{1,0:T(8,128)(2,1)}) custom-call(bf16[1024,768]{1,0:T(8,128)(2,1)} %bitcast.73, bf16[32,288,768]{2,1,0:T(8,128)(2,1)} %bitcast.59, bf16[768,16]{1,0:T(8,128)(2,1)} %slice.189.a_ref, bf16[3,16,768]{2,1,0:T(8,128)(2,1)} %get-tuple-element.99.b_ref, ...), custom_call_target="tpu_custom_call" | custom-call | tf_op jit(solution)/shard_map/qkv/pallas_call | solution.py:104
  254.5 16.0 %attn_fwd.2 = (bf16[1024,768]{1,0:T(8,128)(2,1)}, f32[1024,768]{1,0:T(8,128)}) custom-call(bf16[1024,2304]{1,0:T(8,128)(2,1)} %get-tuple-element.39.q_ref.k_ref.v_ref, bf16[1024,2304]{1,0:T(8,128)(2,1)} %get-tuple-element.39.q_ref.k_ref.v_ref, bf16[1024,2304]{1,0:T(8,128)(2,1)} %get-tuple-element.39.q_ref.k_ref.v_ref), custom_call_target="tpu_custom_call" | custom-call | tf_op jit(solution)/shard_map/attn_fwd/pallas_call | solution.py:154
  270.5 23.1 %ffn_fwd.2 = (bf16[1024,768]{1,0:T(8,128)(2,1)}, bf16[1024,768]{1,0:T(8,128)(2,1)}, f32[1024,1]{1,0:T(8,128)}, bf16[1024,768]{1,0:T(8,128)(2,1)}, f32[1024,1]{1,...) custom-call(bf16[1024,768]{1,0:T(8,128)(2,1)} %bitcast.74, bf16[1024,768]{1,0:T(8,128)(2,1)} %get-tuple-element.40.c_ref, ...), custom_call_target="tpu_custom_call" | custom-call | tf_op jit(solution)/shard_map/ffn_fwd/pallas_call | solution.py:217
  293.7 55.6 %all-gather.8.cloned.1.call-done = bf16[9216,768]{1,0:T(8,128)(2,1)} async-done(((bf16[288,768]{1,0:T(8,128)(2,1)}), bf16[9216,768]{1,0:T(8,128)(2,1)}) %all-gather.8.cloned.1.call-update) | async-done | bytes 14155792 | tf_op jit(solution)/shard_map/all_gather | solution.py:605
  349.3 9.6 %qkv.3 = (bf16[1024,2304]{1,0:T(8,128)(2,1)}, bf16[1024,16]{1,0:T(8,128)(2,1)}, bf16[768,2304]{1,0:T(8,128)(2,1)}) custom-call(bf16[1024,768]{1,0:T(8,128)(2,1)} %get-tuple-element.42.x_ref, bf16[32,288,768]{2,1,0:T(8,128)(2,1)} %bitcast.66, bf16[768,16]{1,0:T(8,128)(2,1)} %slice.204.a_ref, bf16[3,16,768]{2,1,0:T(8,128)(2,1)} %get-tuple-element.98.b_ref, ...), custom_call_target="tpu_custom_call" | custom-call | tf_op jit(solution)/shard_map/qkv/pallas_call | solution.py:104
  358.9 16.0 %attn_fwd.3 = (bf16[1024,768]{1,0:T(8,128)(2,1)}, f32[1024,768]{1,0:T(8,128)}) custom-call(bf16[1024,2304]{1,0:T(8,128)(2,1)} %get-tuple-element.43.q_ref.k_ref.v_ref, bf16[1024,2304]{1,0:T(8,128)(2,1)} %get-tuple-element.43.q_ref.k_ref.v_ref, bf16[1024,2304]{1,0:T(8,128)(2,1)} %get-tuple-element.43.q_ref.k_ref.v_ref), custom_call_target="tpu_custom_call" | custom-call | tf_op jit(solution)/shard_map/attn_fwd/pallas_call | solution.py:154
  375.0 20.5 %ffn_fwd.3 = (bf16[1024,768]{1,0:T(8,128)(2,1)}, bf16[1024,768]{1,0:T(8,128)(2,1)}, f32[1024,1]{1,0:T(8,128)}, bf16[1024,768]{1,0:T(8,128)(2,1)}, f32[1024,1]{1,0:T(8,128)}) custom-call(f32[1024,768]{1,0:T(8,128)} %get-tuple-element.41.h_ref, bf16[1024,768]{1,0:T(8,128)(2,1)} %get-tuple-element.44.c_ref, bf16[32,288,768]{2,1,0:T(8,128)(2,1)} %bitcast.67, ...), custom_call_target="tpu_custom_call" | custom-call | tf_op jit(solution)/shard_map/ffn_fwd/pallas_call | solution.py:217
  395.5 11.7 %ffn_bwd_rows.1 = (f32[160,768]{1,0:T(8,128)}, bf16[160,768]{1,0:T(8,128)(2,1)}) custom-call(s32[2]{0:T(128)} %cnt_ref.1, bf16[160,768]{1,0:T(8,128)(2,1)} %bitcast.80, s32[160,1]{1,0:T(8,128)} %reshape.95.pos_ref, bf16[1024,768]{1,0:T(8,128)(2,1)} %get-tuple-element.46.n1_ref, f32[1024,1]{1,0:T(8,128)} %get-tuple-element.47.s1_ref, ...), custom_call_target="tpu_custom_call" | custom-call | tf_op jit(solution)/shard_map/ffn_bwd_rows/pallas_call | solution.py:291
  407.2 20.0 %attn_bwd_rows.1 = (bf16[160,768]{1,0:T(8,128)(2,1)}, bf16[1024,768]{1,0:T(8,128)(2,1)}, bf16[1024,768]{1,0:T(8,128)(2,1)}, f32[2,16,768]{2,1,0:T(8,128)}, f32[2,16,768]{2,1,0:T(8,128)}) custom-call(bf16[1024,2304]{1,0:T(8,128)(2,1)} %get-tuple-element.43.q_ref.k_ref.v_ref, bf16[1024,2304]{1,0:T(8,128)(2,1)} %get-tuple-element.43.q_ref.k_ref.v_ref, ...), custom_call_target="tpu_custom_call" | custom-call | tf_op jit(solution)/shard_map/attn_bwd_rows/pallas_call | solution.py:357
  427.2 8.4 %dh_rows.1.e_ref = f32[1024,768]{1,0:T(8,128)} custom-call(f32[160,768]{1,0:T(8,128)} %get-tuple-element.50.dr1_ref, bf16[160,768]{1,0:T(8,128)(2,1)} %get-tuple-element.53.dq_ref, bf16[1024,768]{1,0:T(8,128)(2,1)} %get-tuple-element.54.dk_ref, bf16[1024,768]{1,0:T(8,128)(2,1)} %get-tuple-element.55.dv_ref, s32[2,1,80]{2,1,0:T(1,128)} %bitcast.81, ...), custom_call_target="tpu_custom_call" | custom-call | tf_op jit(solution)/shard_map/dh_rows/pallas_call | solution.py:398
  435.6 21.8 %ffn_bwd.1 = (f32[1024,768]{1,0:T(8,128)}, bf16[1024,768]{1,0:T(8,128)(2,1)}) custom-call(f32[1024,768]{1,0:T(8,128)} %dh_rows.1.e_ref, bf16[1024,768]{1,0:T(8,128)(2,1)} %get-tuple-element.57.n1_ref, f32[1024,1]{1,0:T(8,128)} %get-tuple-element.58.s1_ref, bf16[1024,768]{1,0:T(8,128)(2,1)} %get-tuple-element.59.n2_ref, f32[1024,1]{1,0:T(8,128)} %get-tuple-element.60.s2_ref, ...), custom_call_target="tpu_custom_call" | custom-call | tf_op jit(solution)/shard_map/ffn_bwd/pallas_call | solution.py:441
  457.4 26.7 %attn_bwd.1 = (bf16[1024,768]{1,0:T(8,128)(2,1)}, bf16[1024,768]{1,0:T(8,128)(2,1)}, bf16[1024,768]{1,0:T(8,128)(2,1)}, f32[2,16,768]{2,1,0:T(8,128)}, f32[2,16,768]{2,1,0:T(8,128)}) custom-call(bf16[1024,2304]{1,0:T(8,128)(2,1)} %get-tuple-element.39.q_ref.k_ref.v_ref, bf16[1024,2304]{1,0:T(8,128)(2,1)} %get-tuple-element.39.q_ref.k_ref.v_ref, ...), custom_call_target="tpu_custom_call" | custom-call | tf_op jit(solution)/shard_map/attn_bwd/pallas_call | solution.py:496
  484.1 0.9 reduce_sum.36
  485.0 0.9 reduce_sum.37
  486.7 8.9 %dh.1 = f32[1024,768]{1,0:T(8,128)} custom-call(f32[1024,768]{1,0:T(8,128)} %get-tuple-element.62.dr1_ref, bf16[1024,768]{1,0:T(8,128)(2,1)} %get-tuple-element.66.dq_ref, bf16[1024,768]{1,0:T(8,128)(2,1)} %get-tuple-element.67.dk_ref, bf16[1024,768]{1,0:T(8,128)(2,1)} %get-tuple-element.68.dv_ref, bf16[768,2304]{1,0:T(8,128)(2,1)} %get-tuple-element.69.w_ref), custom_call_target="tpu_custom_call" | custom-call | tf_op jit(solution)/shard_map/dh/pallas_call | solution.py:526
  495.7 109.9 %all-reduce.8.cloned.1.call-done = f32[2,16,768]{2,1,0:T(8,128)} async-done(((f32[2,16,768]{2,1,0:T(8,128)}), f32[2,16,768]{2,1,0:T(8,128)}) %all-reduce.8.cloned.1.call-update) | async-done | bytes 98320 | tf_op jit(solution)/shard_map/psum | solution.py:625
  605.6 1.5 fusion.7
  (77 shorter events, 3.9 us)
Async XLA Ops:
  7.2 4.8 copy-start.8
  7.2 4.9 copy-start.5
  7.2 129.2 %all-reduce.10.cloned.1.call-start = ((), (), s32[]{:S(2)}) async-start(), calls=%async_computation.3 | async-start | bytes 172032
  9.2 0.6 copy-start.4
  9.8 235.2 %all-gather.6.cloned.1.call-start = ((), (), s32[]{:S(2)}) async-start(), calls=%async_computation.1 | async-start | bytes 14598144 | tf_op jit(solution)/shard_map/all_gather | solution.py:605
  10.9 2.8 copy-start.9
  10.9 2.8 copy-start.10
  10.9 2.8 copy-start.11
  12.1 0.8 copy-start.3
  12.1 0.9 copy-start.2
  12.9 336.4 %all-gather.8.cloned.1.call-start = ((), (), s32[]{:S(2)}) async-start(), calls=%async_computation.2 | async-start | bytes 14598144 | tf_op jit(solution)/shard_map/all_gather | solution.py:605
  13.7 591.9 %all-reduce.8.cloned.1.call-start = ((), (), s32[]{:S(2)}) async-start(), calls=%async_computation | async-start | bytes 196608 | tf_op jit(solution)/shard_map/psum | solution.py:625
  141.4 113.2 %copy-start.1 = (f32[24,768]{1,0:T(8,128)}, f32[24,768]{1,0:T(8,128)S(1)}, u32[]{:S(2)}) copy-start(f32[24,768]{1,0:T(8,128)S(1)} %convert_bitcast_fusion.par_ref) | copy-start | bytes 221188
  141.4 113.1 %copy-start = (f32[24,768]{1,0:T(8,128)}, f32[24,768]{1,0:T(8,128)S(1)}, u32[]{:S(2)}) copy-start(f32[24,768]{1,0:T(8,128)S(1)} %convert_bitcast_fusion.1.par_ref) | copy-start | bytes 221188
  457.4 28.6 %copy-start.7 = (f32[2,16,768]{2,1,0:T(8,128)S(1)}, f32[2,16,768]{2,1,0:T(8,128)}, u32[]{:S(2)}) copy-start(f32[2,16,768]{2,1,0:T(8,128)} %get-tuple-element.72) | copy-start | bytes 294916
  457.4 28.6 %copy-start.6 = (f32[2,16,768]{2,1,0:T(8,128)S(1)}, f32[2,16,768]{2,1,0:T(8,128)}, u32[]{:S(2)}) copy-start(f32[2,16,768]{2,1,0:T(8,128)} %get-tuple-element.73) | copy-start | bytes 294916
Sparse Core Ops, SparseCore 0:
  14.2 122.1 all-reduce.9
  139.8 105.1 all-gather.5
  247.9 101.3 all-gather.7
  486.9 118.6 all-reduce.7

commit v2 on v1

--- a/solution.py
+++ b/solution.py
@@ -71,18 +71,19 @@
     return jax.ShapeDtypeStruct(shape, dtype)
 
 
-def unit_spec(packed, index):
+def unit_spec(weight, index):
+    packed, base = weight
     nb = packed.shape[0]
-    rb = packed.shape[1] // 12
-    return pl.BlockSpec((nb, rb, D), lambda *g: (0, index(*g), 0))
-
-
-def out_spec(packed, index):
+    return pl.BlockSpec((nb, D // nb, D), lambda *g: (0, base + index(*g), 0))
+
+
+def out_spec(weight, index):
+    packed, base = weight
     nb = packed.shape[0]
-    rb = packed.shape[1] // 12
+    rb = D // nb
     if nb % 4 == 0:
-        return pl.BlockSpec((nb // 4, 4 * rb, D), lambda *g: (index(*g), 2, 0))
-    return pl.BlockSpec((nb, rb, D), lambda *g: (0, 8 + index(*g), 0))
+        return pl.BlockSpec((nb // 4, 4 * rb, D), lambda *g: (index(*g), base, 0))
+    return pl.BlockSpec((nb, rb, D), lambda *g: (0, 4 * base + index(*g), 0))
 
 
 def qkv_kernel(x_ref, w_ref, a_ref, b_ref, bias_ref, o_ref, u_ref, wp_ref):
@@ -99,14 +100,14 @@
         u_ref[...] = nn(x_ref[...], a).astype(BF)
 
 
-def qkv_call(x, packed, down, up3, bias3):
+def qkv_call(x, weights, down, up3, bias3):
     t = x.shape[0]
     return pl.pallas_call(
         qkv_kernel,
         grid=(3,),
         in_specs=[
             whole((t, D)),
-            unit_spec(packed, lambda j: j),
+            unit_spec(weights["qkv"], lambda j: j),
             whole(down.shape),
             pl.BlockSpec((1, 2 * RANK, D), lambda j: (j, 0, 0)),
             pl.BlockSpec((1, 1, D), lambda j: (j, 0, 0)),
@@ -119,7 +120,7 @@
         out_shape=[sds((t, 3 * D), BF), sds((t, 2 * RANK), BF), sds((D, 3 * D), BF)],
         compiler_params=params(),
         name="qkv",
-    )(x, packed, down, up3, bias3)
+    )(x, weights["qkv"][0], down, up3, bias3)
 
 
 PAIRS = H // 2
@@ -207,7 +208,7 @@
                 ho_ref[w, :] = h
 
 
-def ffn_call(h, ctx, packed, par, fb, keep):
+def ffn_call(h, ctx, weights, par, fb, keep):
     t = h.shape[0]
     out_specs = [whole((t, D)), whole((t, D)), whole((t, 1)), whole((t, D)), whole((t, 1))]
     out_shape = [sds((t, D), BF), sds((t, D), BF), sds((t, 1), F32), sds((t, D), BF), sds((t, 1), F32)]
@@ -220,9 +221,9 @@
         in_specs=[
             whole((t, D)),
             whole((t, D)),
-            unit_spec(packed, lambda j: 3),
-            unit_spec(packed, lambda j: 4 + j),
-            out_spec(packed, lambda j: j),
+            unit_spec(weights["o"], lambda j: 0),
+            unit_spec(weights["in"], lambda j: j),
+            out_spec(weights["out"], lambda j: j),
             whole(par.shape),
             pl.BlockSpec((1, D), lambda j: (0, j)),
         ],
@@ -231,7 +232,7 @@
         scratch_shapes=[pltpu.VMEM((t, D), BF), pltpu.VMEM((t, D), F32)],
         compiler_params=params(),
         name="ffn_fwd",
-    )(h, ctx, packed, packed, packed, par, fb)
+    )(h, ctx, weights["o"][0], weights["in"][0], weights["out"][0], par, fb)
 
 
 def pick(pos_ref, s, dtype):
@@ -284,7 +285,7 @@
         dctx_ref[...] = nt(d1.astype(BF), flat(wo_ref)).astype(BF)
 
 
-def ffn_pick_call(cot, pos, counts, n1, s1, n2, s2, packed, par, fb):
+def ffn_pick_call(cot, pos, counts, n1, s1, n2, s2, weights, par, fb):
     t = n1.shape[0]
     seqs = t // LEN
     m = seqs * MAXM
@@ -299,9 +300,9 @@
             whole((t, 1)),
             whole((t, D)),
             whole((t, 1)),
-            unit_spec(packed, lambda j: 3),
-            unit_spec(packed, lambda j: 4 + j),
-            out_spec(packed, lambda j: j),
+            unit_spec(weights["o"], lambda j: 0),
+            unit_spec(weights["in"], lambda j: j),
+            out_spec(weights["out"], lambda j: j),
             whole(par.shape),
             pl.BlockSpec((1, D), lambda j: (0, j)),
         ],
@@ -316,7 +317,7 @@
         ],
         compiler_params=params(),
         name="ffn_bwd_rows",
-    )(counts, cot, pos, n1, s1, n2, s2, packed, packed, packed, par, fb)
+    )(counts, cot, pos, n1, s1, n2, s2, weights["o"][0], weights["in"][0], weights["out"][0], par, fb)
 
 
 def attn_pick_kernel(q_ref, k_ref, v_ref, g_ref, pos_ref, u_ref, dq_ref, dk_ref, dv_ref, gq_ref, gv_ref):
@@ -436,7 +437,7 @@
             dctx_ref[w, :] = nt(d1.astype(BF), wo).astype(BF)
 
 
-def ffn_back_call(e, n1, s1, n2, s2, gp, packed, par):
+def ffn_back_call(e, n1, s1, n2, s2, gp, weights, par):
     t = e.shape[0]
     return pl.pallas_call(
         ffn_back_kernel,
@@ -448,9 +449,9 @@
             whole((t, D)),
             whole((t, 1)),
             pl.BlockSpec((t, D), lambda j: (0, j)),
-            unit_spec(packed, lambda j: 3),
-            unit_spec(packed, lambda j: 4 + j),
-            out_spec(packed, lambda j: j),
+            unit_spec(weights["o"], lambda j: 0),
+            unit_spec(weights["in"], lambda j: j),
+            out_spec(weights["out"], lambda j: j),
             whole(par.shape),
         ],
         out_specs=[whole((t, D)), whole((t, D))],
@@ -458,7 +459,7 @@
         scratch_shapes=[pltpu.VMEM((t, D), BF), pltpu.VMEM((t, D), F32)],
         compiler_params=params(),
         name="ffn_bwd",
-    )(e, n1, s1, n2, s2, gp, packed, packed, packed, par)
+    )(e, n1, s1, n2, s2, gp, weights["o"][0], weights["in"][0], weights["out"][0], par)
 
 
 def attn_back_kernel(q_ref, k_ref, v_ref, g_ref, z_ref, u_ref, dq_ref, dk_ref, dv_ref, gq_ref, gv_ref):
@@ -534,7 +535,7 @@
     )(dr1, dq, dk, dv, wp)
 
 
-def network(tokens, cotangent, positions, counts, packed, smalls, biases, query_up, value_up):
+def network(tokens, cotangent, positions, counts, weights, smalls, biases, query_up, value_up):
     seqs = tokens.shape[0]
     x = tokens.reshape(seqs * LEN, D)
     pos_col = positions.reshape(seqs * MAXM, 1)
@@ -556,9 +557,9 @@
         )
         bias3 = jnp.stack([par[0:1], jnp.zeros((1, D), F32), par[1:2]])
         keep = layer < LAYERS - 1
-        qkv, u, wp = qkv_call(x, packed[layer], down, up3, bias3)
+        qkv, u, wp = qkv_call(x, weights[layer], down, up3, bias3)
         ctx, z = attn_call(qkv)
-        outs = ffn_call(h, ctx, packed[layer], par, biases[layer], keep)
+        outs = ffn_call(h, ctx, weights[layer], par, biases[layer], keep)
         x, n1, s1, n2, s2 = outs[:5]
         gp = None
         if keep:
@@ -569,14 +570,14 @@
     grads = [None] * LAYERS
     qkv, u, wp, z, n1, s1, n2, s2, gp, par = saved[-1]
     dr1, dctx = ffn_pick_call(
-        cot, pos_col, counts, n1, s1, n2, s2, packed[-1], par, biases[-1]
+        cot, pos_col, counts, n1, s1, n2, s2, weights[-1], par, biases[-1]
     )
     dq, dk, dv, gq, gv = attn_pick_call(qkv, dctx, pos_col, u)
     grads[-1] = (gq, gv)
     e = dh_pick_call(dr1, dq, dk, dv, pos_row, wp)
     for layer in reversed(range(LAYERS - 1)):
         qkv, u, wp, z, n1, s1, n2, s2, gp, par = saved[layer]
-        dr1, dctx = ffn_back_call(e, n1, s1, n2, s2, gp, packed[layer], par)
+        dr1, dctx = ffn_back_call(e, n1, s1, n2, s2, gp, weights[layer], par)
         dq, dk, dv, gq, gv = attn_back_call(qkv, dctx, z, u)
         grads[layer] = (gq, gv)
         e = dh_call(dr1, dq, dk, dv, wp)
@@ -588,41 +589,155 @@
     return activations, e.reshape(tokens.shape), out
 
 
+ORDERS = ((8, 2, 16, 4), (16, 4, 8, 2))
+STEPS = 4
+HALF = D // 2
+
+
+def swap_cores(v, n):
+    return lax.ppermute(v, AXES, [(d, d ^ 1) for d in range(n)])
+
+
+def double_step(v, n, step):
+    return lax.ppermute(v, AXES, [(d, d ^ ORDERS[d & 1][step]) for d in range(n)])
+
+
+def gather_pieces(pair, n):
+    held = pair
+    for step in range(STEPS - 1):
+        held = jnp.concatenate([held, double_step(held, n, step)])
+    last = double_step(held, n, STEPS - 1)
+    return held, last, swap_cores(held, n), swap_cores(last, n)
+
+
+def piece_table(me):
+    slot = jnp.arange(16, dtype=jnp.int32)
+
+    def order(core, i):
+        return jnp.where(core == 0, ORDERS[0][i], ORDERS[1][i])
+
+    def held(device):
+        core = device & 1
+        rel = slot & 1
+        for i in range(STEPS - 1):
+            rel = rel + ((slot >> (i + 1)) & 1) * order(core, i)
+        first = device ^ rel
+        return [first, first ^ order(core, STEPS - 1)]
+
+    return jnp.stack(held(me) + held(me ^ 1))
+
+
+def arrange_kernel(table_ref, core_ref, a_ref, b_ref, c_ref, d_ref, o_ref, sem):
+    own = pl.multiple_of(core_ref[0] * HALF, HALF)
+    other = pl.multiple_of(HALF - own, HALF)
+
+    def body(i, carry):
+        for k, (ref, lane) in enumerate(((a_ref, own), (b_ref, own), (c_ref, other), (d_ref, other))):
+            pltpu.make_async_copy(
+                ref.at[i], o_ref.at[table_ref[k, i], :, pl.ds(lane, HALF)], sem
+            ).start()
+        return carry
+
+    lax.fori_loop(0, 16, body, 0)
+    pltpu.make_async_copy(o_ref, o_ref, sem).wait()
+
+
+def arrange_call(table, core, pieces):
+    rows = pieces[0].shape[1]
+    anywhere = pl.BlockSpec(memory_space=pl.ANY)
+    smem = pl.BlockSpec(memory_space=pltpu.SMEM)
+    return pl.pallas_call(
+        arrange_kernel,
+        in_specs=[smem, smem] + [anywhere] * 4,
+        out_specs=anywhere,
+        out_shape=sds((32, rows, D), BF),
+        scratch_shapes=[pltpu.SemaphoreType.DMA],
+        name="arrange",
+    )(table, core, *pieces)
+
+
 def column_blocks(w, n):
     return [w[:, i * D : (i + 1) * D] for i in range(n)]
 
 
+def plain_gather(w_qkv, w_o, w_in, b_in, w_out, small):
+    def gather(v, axis):
+        return lax.all_gather(v, AXES, axis=axis, tiled=True)
+
+    weights, smalls, biases = [], [], []
+    for layer in range(LAYERS):
+        units = column_blocks(gather(w_qkv[layer], 0), 3) + [gather(w_o[layer], 0)]
+        units += column_blocks(gather(w_in[layer], 0), 4) + [gather(w_out[layer], 0)]
+        packed = jnp.concatenate(units)[None]
+        weights.append({"qkv": (packed, 0), "o": (packed, 3), "in": (packed, 4), "out": (packed, 2)})
+        smalls.append(gather(small[layer], 0))
+        biases.append(gather(b_in[layer], 0).reshape(1, FF).astype(F32))
+    return weights, smalls, biases
+
+
+def fast_gather(n, w_qkv, w_o, w_in, b_in, w_out, small):
+    me = lax.axis_index(AXES).astype(jnp.int32)
+    core = me & 1
+    rb = D // n
+    second = lax.all_gather(
+        jnp.concatenate([w_out[1], w_o[1]] + column_blocks(w_in[1], 4)), AXES, axis=0, tiled=False
+    )
+    tiny = jnp.concatenate([small.transpose(1, 0, 2).reshape(rb, -1), b_in.reshape(LAYERS, rb, 4).transpose(1, 0, 2).reshape(rb, -1)], axis=1)
+    tiny = jnp.pad(tiny, ((0, 0), (0, 128 - tiny.shape[1]))).reshape(-1, D)
+    tiny = jnp.pad(tiny, ((0, 8 - tiny.shape[0]), (0, 0)))
+    chunks = [
+        column_blocks(w_qkv[0], 3) + [tiny],
+        [w_o[0]] + column_blocks(w_in[0], 4),
+        [w_out[0]],
+        column_blocks(w_qkv[1], 3),
+    ]
+    sizes = [sum(v.shape[0] for v in c) for c in chunks]
+    rows = jnp.concatenate([v for c in chunks for v in c])
+    first_half, second_half = rows[:, :HALF], rows[:, HALF:]
+    keep = jnp.where(core == 0, first_half, second_half)
+    give = jnp.where(core == 0, second_half, first_half)
+    pairs = jnp.stack([keep, swap_cores(give, n)])
+    table = piece_table(me)
+    packed = []
+    at = 0
+    for size in sizes:
+        packed.append(arrange_call(table, core[None], gather_pieces(pairs[:, at : at + size], n)))
+        at += size
+    weights = [
+        {"qkv": (packed[0], 0), "o": (packed[1], 0), "in": (packed[1], 1), "out": (packed[2], 0)},
+        {"qkv": (packed[3], 0), "o": (second, 4), "in": (second, 5), "out": (second, 0)},
+    ]
+    tiny = packed[0][:, 3 * rb : 3 * rb + rb * 128 // D].reshape(D, 128)
+    width = small.shape[2]
+    smalls = [tiny[:, i * width : (i + 1) * width] for i in range(LAYERS)]
+    at = LAYERS * width
+    biases = [tiny[:, at + 4 * i : at + 4 * i + 4].reshape(1, FF).astype(F32) for i in range(LAYERS)]
+    return weights, smalls, biases
+
+
+def total(v, n):
+    if n & (n - 1):
+        return lax.psum(v, AXES)
+    step = 1
+    while step < n:
+        v = v + lax.ppermute(v, AXES, [(d, d ^ step) for d in range(n)])
+        step *= 2
+    return v
+
+
 def on_device(
-    tokens, cotangent, positions, counts, w_qkv, w_o, w_in, b_in, w_out, small, query_up, value_up
+    sizes, tokens, cotangent, positions, counts, w_qkv, w_o, w_in, b_in, w_out, small, query_up, value_up
 ):
-    packed, smalls, biases = [], [], []
-    for layer in range(LAYERS):
-        shard = jnp.concatenate(
-            column_blocks(w_qkv[layer], 3) + [w_o[layer]] + column_blocks(w_in[layer], 4) + [w_out[layer]]
-        )
-        rb = w_o.shape[1]
-        if rb % 8 == 0:
-            packed.append(lax.all_gather(shard, AXES, axis=0, tiled=False))
-        else:
-            g = lax.all_gather(shard, AXES, axis=0, tiled=False)
-            units = [g[:, i * rb : (i + 1) * rb].reshape(1, D, D) for i in range(8)]
-            units.append(g[:, 8 * rb :].reshape(1, FF, D))
-            packed.append(jnp.concatenate(units, axis=1))
-    tiny = jnp.concatenate(
-        [small.reshape(-1), b_in.reshape(-1)]
+    n = sizes[0] * sizes[1]
+    frozen = (w_qkv, w_o, w_in, b_in, w_out, small)
+    if sizes == (16, 2):
+        weights, smalls, biases = fast_gather(n, *frozen)
+    else:
+        weights, smalls, biases = plain_gather(*frozen)
+    activations, d_tokens, grads = network(
+        tokens, cotangent, positions, counts, weights, smalls, biases, query_up, value_up
     )
-    tiny = lax.all_gather(tiny, AXES, axis=0, tiled=False)
-    n = tiny.shape[0]
-    cut = small.size
-    sm = tiny[:, :cut].reshape(n, LAYERS, -1, small.shape[2])
-    bi = tiny[:, cut:].reshape(n, LAYERS, -1)
-    for layer in range(LAYERS):
-        smalls.append(sm[:, layer].reshape(D, small.shape[2]))
-        biases.append(bi[:, layer].reshape(1, FF).astype(F32))
-    activations, d_tokens, grads = network(
-        tokens, cotangent, positions, counts, packed, smalls, biases, query_up, value_up
-    )
-    g = lax.psum(jnp.stack(grads), AXES)
+    g = total(jnp.stack(grads), n)
     return activations, d_tokens, g[:, :RANK], g[:, RANK:]
 
 
@@ -631,4 +746,7 @@
     mid = P(None, AXES, None)
     in_specs = (both, both, P(AXES, None), P(AXES), mid, mid, mid, P(None, AXES), mid, mid, P(), P())
     out_specs = (both, both, P(), P())
-    return jax.shard_map(on_device, mesh=mesh, in_specs=in_specs, out_specs=out_specs, check_vma=False)
+    sizes = (mesh.shape["dp"], mesh.shape["fsdp"])
+    return jax.shard_map(
+        functools.partial(on_device, sizes), mesh=mesh, in_specs=in_specs, out_specs=out_specs, check_vma=False
+    )

time: 615 us -> 930 us (1.51)
  Pallas kernels: 192 us -> 748 us
  waiting for transfers between devices: 390 us -> 106 us
  starting transfers between devices: 0.16 us -> 30.4 us
    pallas_call x0 -> x4, Pallas kernels: none -> 555 us  [arrange_call(): pl.pallas_call(arrange_kernel, in_specs=[smem, smem] + [anywhere] * 4, ou...]
    all_gather x2 -> x1, waiting for transfers between devices: 159 us -> 0.01 us  [fast_gather(): lax.all_gather(jnp.concatenate([w_out[1], w_o[1]] + column_blocks(w_in[1]...]
    unnamed x5 -> x1, waiting for transfers between devices: 122 us -> 0.02 us
    psum x1 -> x0, waiting for transfers between devices: 110 us -> none  [on_device(): g = lax.psum(jnp.stack(grads), AXES)]
    ppermute x0 -> x30, waiting for transfers between devices: none -> 106 us  [the longest x16 91.4 us: double_step(): lax.ppermute(v, AXES, [(d, d ^ ORDERS[d & 1][step]) for d in range(n)])]
    ppermute x0 -> x30, starting transfers between devices: none -> 30.4 us  [the longest x16 18.5 us: double_step(): lax.ppermute(v, AXES, [(d, d ^ ORDERS[d & 1][step]) for d in range(n)])]
  transfers between devices with their start and end apart: 4 -> 31, of which waited for: 4 -> 14; matrix products, arithmetic and copies ran while one was open for 2% -> 2% of each run, Pallas kernels for 9% -> 69%
where the time goes in v2:
time: 930 us; the launch traced here: 925 us
  Pallas kernels  748 us (80%)
  waiting for transfers between devices  106 us (11%)
  starting transfers between devices  30.4 us (3%)
  between operations  15.1 us (2%)
  local copies, waits for them, and re-layouts  12.9 us (1%)
  other arithmetic  12.7 us (1%)
    pallas_call x4, Pallas kernels, arrange_call(): pl.pallas_call(arrange_kernel, in_specs=[smem, smem] + [anywhere] * 4, ou...  555 us
    ppermute x16, waiting for transfers between devices, double_step(): lax.ppermute(v, AXES, [(d, d ^ ORDERS[d & 1][step]) for d in range(n)])  91.4 us
    pallas_call x2, Pallas kernels, ffn_call(): pl.pallas_call(functools.partial(ffn_kernel, keep), grid=(4,), in_specs=[...  43.4 us
    pallas_call x2, Pallas kernels, attn_call(): pl.pallas_call(attn_kernel, grid=(t // LEN, PAIRS), in_specs=[head_spec(0...  32 us
    pallas_call x1, Pallas kernels, attn_back_call(): pl.pallas_call(attn_back_kernel, grid=(seqs, PAIRS), in_specs=[head_spec(...  26.7 us
    pallas_call x1, Pallas kernels, ffn_back_call(): pl.pallas_call(ffn_back_kernel, grid=(4,), in_specs=[whole((t, D)), whole...  21.6 us
    pallas_call x1, Pallas kernels, attn_pick_call(): pl.pallas_call(attn_pick_kernel, grid=(seqs, PAIRS), in_specs=[head_spec(...  19.9 us
    pallas_call x2, Pallas kernels, qkv_call(): pl.pallas_call(qkv_kernel, grid=(3,), in_specs=[whole((t, D)), unit_spec(...  19.4 us
  transfers between devices with their start and end apart: 31, of which 14 were waited for; matrix products, arithmetic and copies ran while one was open for 2% of the time, Pallas kernels for 69%

profile of v2, /device:TPU:0, one launch (start us, length us, event | category | flops | bytes accessed | tf_op | source)
XLA Modules:
  0.0 925.0 jit_solution(6934482222294651342)
XLA Ops:
  14.7 3.0 collective-permute-start.1
  17.8 3.8 collective-permute-done.1
  21.7 2.1 collective-permute-start.2
  27.9 4.0 collective-permute-done.19
  32.1 3.1 collective-permute-start.3
  35.2 6.3 collective-permute-done.13
  44.8 3.5 collective-permute-done.14
  52.4 19.7 %collective-permute-done.21 = bf16[8,72,384]{2,1,0:T(8,128)(2,1)S(1)} collective-permute-done((bf16[8,72,384]{2,1,0:T(8,128)(2,1)S(1)}, bf16[8,72,384]{2,1,0:T(8,128)(2,1)S(1)}, u32[]{:S(2)}, u32[]{:S(2)}) %collective-permute-start.21) | collective-permute-done | bytes 442400 | tf_op jit(solution)/shard_map/ppermute | solution.py:602
  73.2 2.9 collective-permute-start.23
  76.1 16.4 %collective-permute-done.9 = bf16[8,120,384]{2,1,0:T(8,128)(2,1)S(1)} collective-permute-done((bf16[8,120,384]{2,1,0:T(8,128)(2,1)S(1)}, bf16[8,120,384]{2,1,0:T(8,128)(2,1)S(1)}, u32[]{:S(2)}, u32[]{:S(2)}) %collective-permute-start.9) | collective-permute-done | bytes 737312 | tf_op jit(solution)/shard_map/ppermute | solution.py:602
  94.1 37.0 %collective-permute-done.15 = bf16[8,96,384]{2,1,0:T(8,128)(2,1)} collective-permute-done((bf16[8,96,384]{2,1,0:T(8,128)(2,1)}, bf16[8,96,384]{2,1,0:T(8,128)(2,1)}, u32[]{:S(2)}, u32[]{:S(2)}) %collective-permute-start.15) | collective-permute-done | bytes 589856 | tf_op jit(solution)/shard_map/ppermute | solution.py:602
  141.2 109.2 %arrange.7.w_ref = bf16[32,72,768]{2,1,0:T(8,128)(2,1)} custom-call(s32[4,16]{1,0:T(4,128)} %pad_add_fusion.table_ref, s32[1]{0:T(128)} %bitcast.1.core_ref, bf16[16,72,384]{2,1,0:T(8,128)(2,1)} %pad_maximum_fusion.3.a_ref, bf16[16,72,384]{2,1,0:T(8,128)(2,1)} %collective-permute-done.22.b_ref, bf16[16,72,384]{2,1,0:T(8,128)(2,1)} %collective-permute-done.23.c_ref, ...), custom_call_target="tpu_custom_call" | custom-call | tf_op jit(solution)/shard_map/arrange/pallas_call | solution.py:649
  251.1 120.9 %arrange.4.w_ref = bf16[32,80,768]{2,1,0:T(8,128)(2,1)} custom-call(s32[4,16]{1,0:T(4,128)} %pad_add_fusion.table_ref, s32[1]{0:T(128)} %bitcast.1.core_ref, bf16[16,80,384]{2,1,0:T(8,128)(2,1)} %pad_maximum_fusion.2.a_ref, bf16[16,80,384]{2,1,0:T(8,128)(2,1)} %collective-permute-done.4.b_ref, bf16[16,80,384]{2,1,0:T(8,128)(2,1)} %collective-permute-done.5.c_ref, ...), custom_call_target="tpu_custom_call" | custom-call | tf_op jit(solution)/shard_map/arrange/pallas_call | solution.py:649
  375.2 9.6 %qkv.2 = (bf16[1024,2304]{1,0:T(8,128)(2,1)}, bf16[1024,16]{1,0:T(8,128)(2,1)}, bf16[768,2304]{1,0:T(8,128)(2,1)}) custom-call(bf16[1024,768]{1,0:T(8,128)(2,1)} %bitcast.69, bf16[32,80,768]{2,1,0:T(8,128)(2,1)} %arrange.4.w_ref, bf16[768,16]{1,0:T(8,128)(2,1)} %get-tuple-element.91.a_ref, bf16[3,16,768]{2,1,0:T(8,128)(2,1)} %get-tuple-element.105.b_ref, ...), custom_call_target="tpu_custom_call" | custom-call | tf_op jit(solution)/shard_map/qkv/pallas_call | solution.py:105
  384.8 16.0 %attn_fwd.2 = (bf16[1024,768]{1,0:T(8,128)(2,1)}, f32[1024,768]{1,0:T(8,128)}) custom-call(bf16[1024,2304]{1,0:T(8,128)(2,1)} %get-tuple-element.39.q_ref.k_ref.v_ref, bf16[1024,2304]{1,0:T(8,128)(2,1)} %get-tuple-element.39.q_ref.k_ref.v_ref, bf16[1024,2304]{1,0:T(8,128)(2,1)} %get-tuple-element.39.q_ref.k_ref.v_ref), custom_call_target="tpu_custom_call" | custom-call | tf_op jit(solution)/shard_map/attn_fwd/pallas_call | solution.py:155
  404.4 144.8 %arrange.6.wout_ref = bf16[32,96,768]{2,1,0:T(8,128)(2,1)} custom-call(s32[4,16]{1,0:T(4,128)} %pad_add_fusion.table_ref, s32[1]{0:T(128)} %bitcast.1.core_ref, bf16[16,96,384]{2,1,0:T(8,128)(2,1)} %copy-done.1, bf16[16,96,384]{2,1,0:T(8,128)(2,1)} %collective-permute-done.16.b_ref, bf16[16,96,384]{2,1,0:T(8,128)(2,1)} %collective-permute-done.17.c_ref, ...), custom_call_target="tpu_custom_call" | custom-call | tf_op jit(solution)/shard_map/arrange/pallas_call | solution.py:649
  549.2 180.5 %arrange.5.wo_ref.win_ref = bf16[32,120,768]{2,1,0:T(8,128)(2,1)} custom-call(s32[4,16]{1,0:T(4,128)} %pad_add_fusion.table_ref, s32[1]{0:T(128)} %bitcast.1.core_ref, bf16[16,120,384]{2,1,0:T(8,128)(2,1)} %copy-done, bf16[16,120,384]{2,1,0:T(8,128)(2,1)} %collective-permute-done.10.b_ref, bf16[16,120,384]{2,1,0:T(8,128)(2,1)} %collective-permute-done.11.c_ref, ...), custom_call_target="tpu_custom_call" | custom-call | tf_op jit(solution)/shard_map/arrange/pallas_call | solution.py:649
  729.7 23.0 %ffn_fwd.2 = (bf16[1024,768]{1,0:T(8,128)(2,1)}, bf16[1024,768]{1,0:T(8,128)(2,1)}, f32[1024,1]{1,0:T(8,128)}, bf16[1024,768]{1,0:T(8,128)(2,1)}, f32[1024,1]{1,...) custom-call(bf16[1024,768]{1,0:T(8,128)(2,1)} %bitcast.70, bf16[1024,768]{1,0:T(8,128)(2,1)} %get-tuple-element.40.c_ref, ...), custom_call_target="tpu_custom_call" | custom-call | tf_op jit(solution)/shard_map/ffn_fwd/pallas_call | solution.py:218
  752.7 9.8 %qkv.3 = (bf16[1024,2304]{1,0:T(8,128)(2,1)}, bf16[1024,16]{1,0:T(8,128)(2,1)}, bf16[768,2304]{1,0:T(8,128)(2,1)}) custom-call(bf16[1024,768]{1,0:T(8,128)(2,1)} %get-tuple-element.42.x_ref, bf16[32,72,768]{2,1,0:T(8,128)(2,1)} %arrange.7.w_ref, bf16[768,16]{1,0:T(8,128)(2,1)} %get-tuple-element.90.a_ref, bf16[3,16,768]{2,1,0:T(8,128)(2,1)} %get-tuple-element.104.b_ref, ...), custom_call_target="tpu_custom_call" | custom-call | tf_op jit(solution)/shard_map/qkv/pallas_call | solution.py:105
  762.6 16.0 %attn_fwd.3 = (bf16[1024,768]{1,0:T(8,128)(2,1)}, f32[1024,768]{1,0:T(8,128)}) custom-call(bf16[1024,2304]{1,0:T(8,128)(2,1)} %get-tuple-element.43.q_ref.k_ref.v_ref, bf16[1024,2304]{1,0:T(8,128)(2,1)} %get-tuple-element.43.q_ref.k_ref.v_ref, bf16[1024,2304]{1,0:T(8,128)(2,1)} %get-tuple-element.43.q_ref.k_ref.v_ref), custom_call_target="tpu_custom_call" | custom-call | tf_op jit(solution)/shard_map/attn_fwd/pallas_call | solution.py:155
  778.6 20.3 %ffn_fwd.3 = (bf16[1024,768]{1,0:T(8,128)(2,1)}, bf16[1024,768]{1,0:T(8,128)(2,1)}, f32[1024,1]{1,0:T(8,128)}, bf16[1024,768]{1,0:T(8,128)(2,1)}, f32[1024,1]{1,0:T(8,128)}) custom-call(f32[1024,768]{1,0:T(8,128)} %get-tuple-element.41.h_ref, bf16[1024,768]{1,0:T(8,128)(2,1)} %get-tuple-element.44.c_ref, bf16[32,216,768]{2,1,0:T(8,128)(2,1)} %bitcast.63, ...), custom_call_target="tpu_custom_call" | custom-call | tf_op jit(solution)/shard_map/ffn_fwd/pallas_call | solution.py:218
  798.9 11.7 %ffn_bwd_rows.1 = (f32[160,768]{1,0:T(8,128)}, bf16[160,768]{1,0:T(8,128)(2,1)}) custom-call(s32[2]{0:T(128)} %cnt_ref.1, bf16[160,768]{1,0:T(8,128)(2,1)} %bitcast.76, s32[160,1]{1,0:T(8,128)} %reshape.182.pos_ref, bf16[1024,768]{1,0:T(8,128)(2,1)} %get-tuple-element.46.n1_ref, f32[1024,1]{1,0:T(8,128)} %get-tuple-element.47.s1_ref, ...), custom_call_target="tpu_custom_call" | custom-call | tf_op jit(solution)/shard_map/ffn_bwd_rows/pallas_call | solution.py:292
  810.6 19.9 %attn_bwd_rows.1 = (bf16[160,768]{1,0:T(8,128)(2,1)}, bf16[1024,768]{1,0:T(8,128)(2,1)}, bf16[1024,768]{1,0:T(8,128)(2,1)}, f32[2,16,768]{2,1,0:T(8,128)}, f32[2,16,768]{2,1,0:T(8,128)}) custom-call(bf16[1024,2304]{1,0:T(8,128)(2,1)} %get-tuple-element.43.q_ref.k_ref.v_ref, bf16[1024,2304]{1,0:T(8,128)(2,1)} %get-tuple-element.43.q_ref.k_ref.v_ref, ...), custom_call_target="tpu_custom_call" | custom-call | tf_op jit(solution)/shard_map/attn_bwd_rows/pallas_call | solution.py:358
  830.5 8.7 dh_rows.1.e_ref
  839.2 21.6 %ffn_bwd.1 = (f32[1024,768]{1,0:T(8,128)}, bf16[1024,768]{1,0:T(8,128)(2,1)}) custom-call(f32[1024,768]{1,0:T(8,128)} %dh_rows.1.e_ref, bf16[1024,768]{1,0:T(8,128)(2,1)} %get-tuple-element.57.n1_ref, f32[1024,1]{1,0:T(8,128)} %get-tuple-element.58.s1_ref, bf16[1024,768]{1,0:T(8,128)(2,1)} %get-tuple-element.59.n2_ref, f32[1024,1]{1,0:T(8,128)} %get-tuple-element.60.s2_ref, ...), custom_call_target="tpu_custom_call" | custom-call | tf_op jit(solution)/shard_map/ffn_bwd/pallas_call | solution.py:442
  860.9 26.7 %attn_bwd.1 = (bf16[1024,768]{1,0:T(8,128)(2,1)}, bf16[1024,768]{1,0:T(8,128)(2,1)}, bf16[1024,768]{1,0:T(8,128)(2,1)}, f32[2,16,768]{2,1,0:T(8,128)}, f32[2,16,768]{2,1,0:T(8,128)}) custom-call(bf16[1024,2304]{1,0:T(8,128)(2,1)} %get-tuple-element.39.q_ref.k_ref.v_ref, bf16[1024,2304]{1,0:T(8,128)(2,1)} %get-tuple-element.39.q_ref.k_ref.v_ref, ...), custom_call_target="tpu_custom_call" | custom-call | tf_op jit(solution)/shard_map/attn_bwd/pallas_call | solution.py:497
  890.9 2.4 collective-permute-start.26
  893.3 3.3 collective-permute-done.26
  898.0 3.4 collective-permute-done.27
  902.1 4.0 collective-permute-done.28
  906.1 2.1 collective-permute-start.29
  908.1 8.9 dh.1
  (160 shorter events, 45.2 us)
Async XLA Ops:
  7.2 771.4 %all-gather.3.cloned.1.call-start = ((), (), s32[]{:S(2)}) async-start(), calls=%async_computation | async-start | bytes 10948608 | tf_op jit(solution)/shard_map/all_gather | solution.py:682
  13.0 1.7 collective-permute-start
  14.7 7.0 collective-permute-start.1
  17.7 8.2 collective-permute-start.7
  21.7 10.3 %collective-permute-start.2 = (bf16[4,80,384]{2,1,0:T(8,128)(2,1)S(1)}, bf16[4,80,384]{2,1,0:T(8,128)(2,1)S(1)}, u32[]{:S(2)}, u32[]{:S(2)}) collective-permute-start(bf16[4,80,384]{2,1,0:T(8,128)(2,1)S(1)} %pad_maximum_fusion.10), channel_id=1, source_target_pairs={{0,2},{1,5},{2,0},{3,7},{4,6},{5,1},{6,4},{7,3},{8,10},{9,13},{10,... | collective-permute-start | bytes 737288 | tf_op jit(solution)/shard_map/ppermute | solution.py:602
  23.9 8.1 collective-permute-start.19
  25.4 16.1 %collective-permute-start.13 = (bf16[2,96,384]{2,1,0:T(8,128)(2,1)S(1)}, bf16[2,96,384]{2,1,0:T(8,128)(2,1)S(1)}, u32[]{:S(2)}, u32[]{:S(2)}) collective-permute-start(bf16[2,96,384]{2,1,0:T(8,128)(2,1)S(1)} %pad_maximum_fusion.13), channel_id=1, source_target_pairs={{0,8},{1,17},{2,10},{3,19},{4,12},{5,21},{6,14},{7,23},{8,0},{9,25... | collective-permute-start | bytes 442376 | tf_op jit(solution)/shard_map/ppermute | solution.py:602
  26.0 16.7 %collective-permute-start.8 = (bf16[4,120,384]{2,1,0:T(8,128)(2,1)S(1)}, bf16[4,120,384]{2,1,0:T(8,128)(2,1)S(1)}, u32[]{:S(2)}, u32[]{:S(2)}) collective-permute-start(bf16[4,120,384]{2,1,0:T(8,128)(2,1)S(1)} %pad_maximum_fusion.8), channel_id=1, source_target_pairs={{0,2},{1,5},{2,0},{3,7},{4,6},{5,1},{6,4},{7,3},{8,10},{9,13},{10,... | collective-permute-start | bytes 1105928 | tf_op jit(solution)/shard_map/ppermute | solution.py:602
  32.0 9.6 %collective-permute-start.20 = (bf16[4,72,384]{2,1,0:T(8,128)(2,1)S(1)}, bf16[4,72,384]{2,1,0:T(8,128)(2,1)S(1)}, u32[]{:S(2)}, u32[]{:S(2)}) collective-permute-start(bf16[4,72,384]{2,1,0:T(8,128)(2,1)S(1)} %pad_maximum_fusion.11), channel_id=1, source_target_pairs={{0,2},{1,5},{2,0},{3,7},{4,6},{5,1},{6,4},{7,3},{8,10},{9,13},{10,... | collective-permute-start | bytes 663560 | tf_op jit(solution)/shard_map/ppermute | solution.py:602
  32.1 17.7 %collective-permute-start.3 = (bf16[8,80,384]{2,1,0:T(8,128)(2,1)S(1)}, bf16[8,80,384]{2,1,0:T(8,128)(2,1)S(1)}, u32[]{:S(2)}, u32[]{:S(2)}) collective-permute-start(bf16[8,80,384]{2,1,0:T(8,128)(2,1)S(1)} %pad_maximum_fusion.6), channel_id=1, source_target_pairs={{0,16},{1,9},{2,18},{3,11},{4,20},{5,13},{6,22},{7,15},{8,24},{9,1... | collective-permute-start | bytes 1474568 | tf_op jit(solution)/shard_map/ppermute | solution.py:602
  41.5 6.8 collective-permute-start.14
  41.7 30.5 %collective-permute-start.21 = (bf16[8,72,384]{2,1,0:T(8,128)(2,1)S(1)}, bf16[8,72,384]{2,1,0:T(8,128)(2,1)S(1)}, u32[]{:S(2)}, u32[]{:S(2)}) collective-permute-start(bf16[8,72,384]{2,1,0:T(8,128)(2,1)S(1)} %pad_maximum_fusion.7), channel_id=1, source_target_pairs={{0,16},{1,9},{2,18},{3,11},{4,20},{5,13},{6,22},{7,15},{8,24},{9,1... | collective-permute-start | bytes 1327112 | tf_op jit(solution)/shard_map/ppermute | solution.py:602
  42.8 49.6 %collective-permute-start.9 = (bf16[8,120,384]{2,1,0:T(8,128)(2,1)S(1)}, bf16[8,120,384]{2,1,0:T(8,128)(2,1)S(1)}, u32[]{:S(2)}, u32[]{:S(2)}) collective-permute-start(bf16[8,120,384]{2,1,0:T(8,128)(2,1)S(1)} %pad_maximum_fusion.4), channel_id=1, source_target_pairs={{0,16},{1,9},{2,18},{3,11},{4,20},{5,13},{6,22},{7,15},{8,24},{9,1... | collective-permute-start | bytes 2211848 | tf_op jit(solution)/shard_map/ppermute | solution.py:602
  49.2 82.0 %collective-permute-start.15 = (bf16[8,96,384]{2,1,0:T(8,128)(2,1)}, bf16[8,96,384]{2,1,0:T(8,128)(2,1)}, u32[]{:S(2)}, u32[]{:S(2)}) collective-permute-start(bf16[8,96,384]{2,1,0:T(8,128)(2,1)} %pad_maximum_fusion.5), channel_id=1, source_target_pairs={{0,16},{1,9},{2,18},{3,11},{4,20},{5,13},{6,22},{7,15},{8,24},{9,1... | collective-permute-start | bytes 1769480 | tf_op jit(solution)/shard_map/ppermute | solution.py:602
  50.9 84.0 %collective-permute-start.4 = (bf16[16,80,384]{2,1,0:T(8,128)(2,1)}, bf16[16,80,384]{2,1,0:T(8,128)(2,1)}, u32[]{:S(2)}, u32[]{:S(2)}) collective-permute-start(bf16[16,80,384]{2,1,0:T(8,128)(2,1)} %pad_maximum_fusion.2.a_ref), channel_id=1, source_target_pairs={{0,4},{1,3},{2,6},{3,1},{4,0},{5,7},{6,2},{7,5},{8,12},{9,11},{10,... | collective-permute-start | bytes 2949128 | tf_op jit(solution)/shard_map/ppermute | solution.py:602
  73.2 61.7 %collective-permute-start.22 = (bf16[16,72,384]{2,1,0:T(8,128)(2,1)}, bf16[16,72,384]{2,1,0:T(8,128)(2,1)}, u32[]{:S(2)}, u32[]{:S(2)}) collective-permute-start(bf16[16,72,384]{2,1,0:T(8,128)(2,1)} %pad_maximum_fusion.3.a_ref), channel_id=1, source_target_pairs={{0,4},{1,3},{2,6},{3,1},{4,0},{5,7},{6,2},{7,5},{8,12},{9,11},{10,... | collective-permute-start | bytes 2654216 | tf_op jit(solution)/shard_map/ppermute | solution.py:602
  73.2 62.9 %collective-permute-start.23 = (bf16[16,72,384]{2,1,0:T(8,128)(2,1)}, bf16[16,72,384]{2,1,0:T(8,128)(2,1)}, u32[]{:S(2)}, u32[]{:S(2)}) collective-permute-start(bf16[16,72,384]{2,1,0:T(8,128)(2,1)} %pad_maximum_fusion.3.a_ref), channel_id=1, source_target_pairs={{0,1},{1,0},{2,3},{3,2},{4,5},{5,4},{6,7},{7,6},{8,9},{9,8},{10,11... | collective-permute-start | bytes 2654216 | tf_op jit(solution)/shard_map/ppermute | solution.py:598
  92.6 157.7 %copy-start = (bf16[16,120,384]{2,1,0:T(8,128)(2,1)}, bf16[16,120,384]{2,1,0:T(8,128)(2,1)S(1)}, u32[]{:S(2)}) copy-start(bf16[16,120,384]{2,1,0:T(8,128)(2,1)S(1)} %pad_maximum_fusion.a_ref) | copy-start | bytes 4423684
  92.7 158.3 %collective-permute-start.10 = (bf16[16,120,384]{2,1,0:T(8,128)(2,1)S(1)}, bf16[16,120,384]{2,1,0:T(8,128)(2,1)}, u32[]{:S(2)}, u32[]{:S(2)}) collective-permute-start(bf16[16,120,384]{2,1,0:T(8,128)(2,1)S(1)} %pad_maximum_fusion.a_ref), channel_id=1, source_target_pairs={{0,4},{1,3},{2,6},{3,1},{4,0},{5,7},{6,2},{7,5},{8,12},{9,11},{10,... | collective-permute-start | bytes 4423688 | tf_op jit(solution)/shard_map/ppermute | solution.py:602
  132.4 118.2 %collective-permute-start.16 = (bf16[16,96,384]{2,1,0:T(8,128)(2,1)S(1)}, bf16[16,96,384]{2,1,0:T(8,128)(2,1)}, u32[]{:S(2)}, u32[]{:S(2)}) collective-permute-start(bf16[16,96,384]{2,1,0:T(8,128)(2,1)S(1)} %pad_maximum_fusion.1.a_ref), channel_id=1, source_target_pairs={{0,4},{1,3},{2,6},{3,1},{4,0},{5,7},{6,2},{7,5},{8,12},{9,11},{10,... | collective-permute-start | bytes 3538952 | tf_op jit(solution)/shard_map/ppermute | solution.py:602
  134.9 115.5 %collective-permute-start.5 = (bf16[16,80,384]{2,1,0:T(8,128)(2,1)}, bf16[16,80,384]{2,1,0:T(8,128)(2,1)}, u32[]{:S(2)}, u32[]{:S(2)}) collective-permute-start(bf16[16,80,384]{2,1,0:T(8,128)(2,1)} %pad_maximum_fusion.2.a_ref), channel_id=1, source_target_pairs={{0,1},{1,0},{2,3},{3,2},{4,5},{5,4},{6,7},{7,6},{8,9},{9,8},{10,11... | collective-permute-start | bytes 2949128 | tf_op jit(solution)/shard_map/ppermute | solution.py:598
  135.0 116.1 %collective-permute-start.6 = (bf16[16,80,384]{2,1,0:T(8,128)(2,1)}, bf16[16,80,384]{2,1,0:T(8,128)(2,1)}, u32[]{:S(2)}, u32[]{:S(2)}) collective-permute-start(bf16[16,80,384]{2,1,0:T(8,128)(2,1)} %collective-permute-done.4.b_ref), channel_id=1, source_target_pairs={{0,1},{1,0},{2,3},{3,2},{4,5},{5,4},{6,7},{7,6},{8,9},{9,8},{10,11... | collective-permute-start | bytes 2949128 | tf_op jit(solution)/shard_map/ppermute | solution.py:598
  136.1 4.2 collective-permute-start.24
  140.2 264.1 %collective-permute-start.17 = (bf16[16,96,384]{2,1,0:T(8,128)(2,1)S(1)}, bf16[16,96,384]{2,1,0:T(8,128)(2,1)}, u32[]{:S(2)}, u32[]{:S(2)}) collective-permute-start(bf16[16,96,384]{2,1,0:T(8,128)(2,1)S(1)} %pad_maximum_fusion.1.a_ref), channel_id=1, source_target_pairs={{0,1},{1,0},{2,3},{3,2},{4,5},{5,4},{6,7},{7,6},{8,9},{9,8},{10,11... | collective-permute-start | bytes 3538952 | tf_op jit(solution)/shard_map/ppermute | solution.py:598
  250.4 298.8 %collective-permute-start.11 = (bf16[16,120,384]{2,1,0:T(8,128)(2,1)S(1)}, bf16[16,120,384]{2,1,0:T(8,128)(2,1)}, u32[]{:S(2)}, u32[]{:S(2)}) collective-permute-start(bf16[16,120,384]{2,1,0:T(8,128)(2,1)S(1)} %pad_maximum_fusion.a_ref), channel_id=1, source_target_pairs={{0,1},{1,0},{2,3},{3,2},{4,5},{5,4},{6,7},{7,6},{8,9},{9,8},{10,11... | collective-permute-start | bytes 4423688 | tf_op jit(solution)/shard_map/ppermute | solution.py:598
  250.6 153.8 %collective-permute-start.18 = (bf16[16,96,384]{2,1,0:T(8,128)(2,1)}, bf16[16,96,384]{2,1,0:T(8,128)(2,1)}, u32[]{:S(2)}, u32[]{:S(2)}) collective-permute-start(bf16[16,96,384]{2,1,0:T(8,128)(2,1)} %collective-permute-done.16.b_ref), channel_id=1, source_target_pairs={{0,1},{1,0},{2,3},{3,2},{4,5},{5,4},{6,7},{7,6},{8,9},{9,8},{10,11... | collective-permute-start | bytes 3538952 | tf_op jit(solution)/shard_map/ppermute | solution.py:598
  251.0 298.2 %collective-permute-start.12 = (bf16[16,120,384]{2,1,0:T(8,128)(2,1)}, bf16[16,120,384]{2,1,0:T(8,128)(2,1)}, u32[]{:S(2)}, u32[]{:S(2)}) collective-permute-start(bf16[16,120,384]{2,1,0:T(8,128)(2,1)} %collective-permute-done.10.b_ref), channel_id=1, source_target_pairs={{0,1},{1,0},{2,3},{3,2},{4,5},{5,4},{6,7},{7,6},{8,9},{9,8},{10,11... | collective-permute-start | bytes 4423688 | tf_op jit(solution)/shard_map/ppermute | solution.py:598
  889.5 1.4 collective-permute-start.25
  890.9 5.7 collective-permute-start.26
  896.7 4.7 collective-permute-start.27
  901.4 4.7 collective-permute-start.28
  906.1 11.0 %collective-permute-start.29 = (f32[2,16,768]{2,1,0:T(8,128)S(1)}, f32[2,16,768]{2,1,0:T(8,128)S(1)}, u32[]{:S(2)}, u32[]{:S(2)}) collective-permute-start(f32[2,16,768]{2,1,0:T(8,128)S(1)} %add.124), channel_id=1, source_target_pairs={{0,16},{1,17},{2,18},{3,19},{4,20},{5,21},{6,22},{7,23},{8,24},{9,... | collective-permute-start | bytes 294920 | tf_op jit(solution)/shard_map/ppermute | solution.py:723
  (12 other events, 330.8 us)
Sparse Core Ops, SparseCore 0:
  13.0 120.1 all-gather.2
